TPU v7x, 768 devices: a whole 4x8x12 slice. The times are simulated.
768 devices in a mesh: seq: 48 (over z_lo, y, core), head: 16 (over z_hi, x).
Axes of the slice: x: 4, y: 8, z: 12 (z_hi: 4, z_lo: 3; z = z_hi * 3 + z_lo), core: 2. Of those that a mesh axis runs over, the one named last changes fastest.
Arguments:
- queries: bfloat16 [24576, 4096], P('seq', 'head'), may hold values from -16 to 16
- keys: bfloat16 [24576, 4096], P('seq', 'head'), may hold values from -16 to 16
- values: bfloat16 [24576, 4096], P('seq', 'head'), may hold values from -6 to 6
- segment_ids: int32 [24576], P('seq'), may hold values from 0 to 31, never falling along the last dimension, each value on 1 to 1024 neighbouring positions
- out_weight: bfloat16 [4096, 5120], P('head'), may hold values from -0.125 to 0.125
Outputs:
- mixed: bfloat16 [24576, 5120], P('seq', 'head')
Inputs may be any that keep to these rules, and one draw needn't show every extreme that they name: `segment_ids`: segment numbers never fall along the sequence; a segment holds at most 1024 tokens.
All inputs are finite; a program needn't handle non-finite values.
Results may differ from a plain program's by a relative error of at most 0.02.
Values may be sent and summed in bfloat16 or wider, within the bound.
A program may use at most 64 MiB of HBM per device.

v0:
```python
import jax
import jax.numpy as jnp
from jax import lax
from jax.sharding import Mesh
from jax.sharding import PartitionSpec as P

HEAD_DEV = 2
SPAN = 2
HEAD = ("head_0", "head_1")


def shifted(block, axis, distance):
    devices = range(lax.axis_size(axis))
    route = [(i - distance, i) for i in devices if i - distance in devices]
    return lax.ppermute(block, axis, route)


def reduced_to_own(pieces, axes, sequence):
    inside = pieces.shape[1:]
    pieces = pieces.reshape(*(lax.axis_size(a) for a in axes), *inside)
    pieces = jnp.moveaxis(pieces, sequence, range(len(axes))).reshape(-1, *inside)
    for k in sequence:
        pieces = lax.psum_scatter(pieces, axes[k], scatter_dimension=0, tiled=True)
    return pieces[0]


def cut_along(array, dim, devices):
    before, after = (array.shape[:dim], array.shape[dim + 1 :])
    return jnp.moveaxis(array.reshape(*before, devices, -1, *after), dim, 0)


def summed_rows(array, axes, sequence, dim):
    devices = lax.axis_size(axes)
    return reduced_to_own(cut_along(array, dim, devices), axes, sequence)


def attend(query, query_marks, key_rows, value_rows, key_marks):
    rows = query.shape[0]
    head_size = query.shape[1] // HEAD_DEV
    query_heads = query.reshape(rows, HEAD_DEV, head_size)
    key_heads = key_rows.reshape(key_rows.shape[0], HEAD_DEV, head_size)
    value_heads = value_rows.reshape(value_rows.shape[0], HEAD_DEV, head_size)
    allowed = (query_marks[:, None] == key_marks[None, :])[None]
    scores = jnp.einsum(
        "qhd,khd->hqk", query_heads, key_heads, preferred_element_type=jnp.float32
    ) * head_size ** (-0.5)
    scores = jnp.where(allowed, scores, -1e30)
    peak = jnp.max(scores, axis=2)
    weights = jnp.where(allowed, jnp.exp(scores - peak[:, :, None]), 0.0)
    total = jnp.sum(weights, axis=2)
    summed = jnp.einsum(
        "hqk,khd->qhd",
        weights.astype(jnp.bfloat16),
        value_heads,
        preferred_element_type=jnp.float32,
    )
    return (summed, peak, total)


def attend_block(query, query_marks, key_rows, value_rows, key_marks):
    return attend(query, query_marks, key_rows, value_rows, key_marks)


def combine(first, second):
    peak = jnp.maximum(first[1], second[1])
    scale_one = jnp.exp(first[1] - peak)
    scale_two = jnp.exp(second[1] - peak)
    summed = (
        first[0] * jnp.transpose(scale_one)[:, :, None]
        + second[0] * jnp.transpose(scale_two)[:, :, None]
    )
    return (summed, peak, first[2] * scale_one + second[2] * scale_two)


def pull_keys(query, marks, key_rows, value_rows, offset):
    far_keys, far_values, far_marks = shifted((key_rows, value_rows, marks), "seq", offset)
    return attend_block(query, marks, far_keys, far_values, far_marks)


def shards(queries, keys, values, segment_ids, out_weight):
    marks = segment_ids + 1
    state = attend_block(queries, marks, keys, values, marks)
    for distance in range(1, SPAN + 1):
        for sign in (1, -1):
            state = combine(state, pull_keys(queries, marks, keys, values, sign * distance))
    summed, peak, total = state
    attended = (
        (summed / jnp.transpose(total)[:, :, None])
        .reshape(queries.shape[0], queries.shape[1])
        .astype(jnp.bfloat16)
    )
    term = jnp.dot(attended, out_weight, preferred_element_type=jnp.float32)
    mixed = summed_rows(term.astype(jnp.bfloat16), HEAD, (1, 0), 1).astype(jnp.float32)
    return mixed.astype(jnp.bfloat16)


def solution(mesh):
    torus = Mesh(mesh.devices.reshape(mesh.shape["seq"], 4, 4), ("seq", "head_0", "head_1"))
    in_specs = (P("seq", HEAD), P("seq", HEAD), P("seq", HEAD), P("seq"), P(HEAD, None))
    out_specs = P("seq", HEAD)
    return jax.shard_map(
        shards, mesh=torus, in_specs=in_specs, out_specs=out_specs, check_vma=False
    )
```

profile of v0, /device:TPU:1, one launch (start us, length us, event | category | flops | bytes accessed | tf_op | source)
XLA Modules:
  0.0 239.9 jit_solution(11918863710439203750)
XLA Ops:
  6.5 0.0 copy-start
  6.5 0.0 reduce-scatter.3.cloned.1.call-start
  6.5 0.8 broadcast_add_fusion
  7.4 4.6 %collective-permute-start = (s32[512]{0:T(512)S(1)}, s32[512]{0:T(512)S(1)}, u32[]{:S(2)}, u32[]{:S(2)}) collective-permute-start(s32[512]{0:T(512)S(1)} %broadcast_add_fusion), channel_id=1, source_target_pairs={{0,16},{16,32},{32,48},{48,64},{64,80},{80,96},{96,112},{112,128},... | collective-permute-start | bytes 6152 | tf_op jit(solution)/shard_map/ppermute | solution.py:15
  12.0 9.1 %collective-permute-start.3 = (s32[512]{0:T(512)S(1)}, s32[512]{0:T(512)S(1)}, u32[]{:S(2)}, u32[]{:S(2)}) collective-permute-start(s32[512]{0:T(512)S(1)} %broadcast_add_fusion), channel_id=1, source_target_pairs={{16,0},{32,16},{48,32},{64,48},{80,64},{96,80},{112,96},{128,112},... | collective-permute-start | bytes 6152 | tf_op jit(solution)/shard_map/ppermute | solution.py:15
  21.1 1.3 collective-permute-start.6
  22.4 1.3 collective-permute-start.9
  23.6 1.8 copy.52
  25.5 3.5 %collective-permute-start.1 = (bf16[512,256]{0,1:T(8,128)(2,1)}, bf16[512,256]{0,1:T(8,128)(2,1)}, u32[]{:S(2)}, u32[]{:S(2)}) collective-permute-start(bf16[512,256]{0,1:T(8,128)(2,1)} %copy.52), channel_id=1, source_target_pairs={{0,16},{16,32},{32,48},{48,64},{64,80},{80,96},{96,112},{112,128},... | collective-permute-start | bytes 786440 | tf_op jit(solution)/shard_map/ppermute | solution.py:15
  29.0 1.8 copy.83
  30.8 0.0 collective-permute-done
  30.8 2.5 %collective-permute-start.7 = (bf16[512,256]{0,1:T(8,128)(2,1)}, bf16[512,256]{0,1:T(8,128)(2,1)S(1)}, u32[]{:S(2)}, u32[]{:S(2)}) collective-permute-start(bf16[512,256]{0,1:T(8,128)(2,1)} %copy.52), channel_id=1, source_target_pairs={{0,32},{16,48},{32,64},{48,80},{64,96},{80,112},{96,128},{112,144}... | collective-permute-start | bytes 786440 | tf_op jit(solution)/shard_map/ppermute | solution.py:15
  33.3 0.0 collective-permute-done.3
  33.3 2.7 %collective-permute-start.4 = (bf16[512,256]{0,1:T(8,128)(2,1)}, bf16[512,256]{0,1:T(8,128)(2,1)S(1)}, u32[]{:S(2)}, u32[]{:S(2)}) collective-permute-start(bf16[512,256]{0,1:T(8,128)(2,1)} %copy.52), channel_id=1, source_target_pairs={{16,0},{32,16},{48,32},{64,48},{80,64},{96,80},{112,96},{128,112},... | collective-permute-start | bytes 786440 | tf_op jit(solution)/shard_map/ppermute | solution.py:15
  36.0 0.0 collective-permute-done.6
  36.0 1.3 collective-permute-start.10
  37.3 0.0 collective-permute-done.9
  37.3 3.5 %collective-permute-start.2 = (bf16[512,256]{1,0:T(8,128)(2,1)}, bf16[512,256]{1,0:T(8,128)(2,1)}, u32[]{:S(2)}, u32[]{:S(2)}) collective-permute-start(bf16[512,256]{1,0:T(8,128)(2,1)} %param.7), channel_id=1, source_target_pairs={{0,16},{16,32},{32,48},{48,64},{64,80},{80,96},{96,112},{112,128},... | collective-permute-start | bytes 786440 | tf_op jit(solution)/shard_map/ppermute | solution.py:15
  40.9 0.9 broadcast_compare_fusion.3
  41.8 0.0 copy-start.5
  41.8 1.7 fusion
  43.4 0.0 collective-permute-done.1
  43.5 1.9 collective-permute-start.5
  45.4 0.0 copy-done.7
  45.4 1.6 fusion.1
  47.0 0.0 copy-start.3
  47.0 0.0 collective-permute-done.7
  47.0 4.3 %collective-permute-start.8 = (bf16[512,256]{1,0:T(8,128)(2,1)}, bf16[512,256]{1,0:T(8,128)(2,1)}, u32[]{:S(2)}, u32[]{:S(2)}) collective-permute-start(bf16[512,256]{1,0:T(8,128)(2,1)} %param.7), channel_id=1, source_target_pairs={{0,32},{16,48},{32,64},{48,80},{64,96},{80,112},{96,128},{112,144}... | collective-permute-start | bytes 786440 | tf_op jit(solution)/shard_map/ppermute | solution.py:15
  51.4 0.6 fusion.3
  52.0 0.0 copy-start.2
  52.0 0.0 collective-permute-done.4
  52.0 1.5 collective-permute-start.11
  53.5 0.6 fusion.2
  54.1 0.0 copy-start.4
  54.1 0.0 collective-permute-done.10
  54.1 0.6 fusion.4
  54.8 1.3 copy-done.1
  56.1 0.6 fusion.13
  56.7 0.0 copy-done.5
  56.7 1.1 fusion.5
  57.8 0.0 copy-start.6
  57.8 1.1 fusion.9
  59.0 0.0 copy-done.6
  59.0 1.6 fusion.23
  60.6 0.0 collective-permute-done.2
  60.6 1.8 copy.55
  62.4 3.5 %fusion.24 = f32[512,2,128]{0,2,1:T(8,128)} fusion(f32[512,2,128]{0,2,1:T(8,128)} %fusion.23, bf16[512,2,128]{0,2,1:T(8,128)(2,1)} %bitcast.211, f32[2,512,512]{1,2,0:T(8,128)} %copy-done.3, f32[2,512]{1,0:T(2,128)S(1)} %get-tuple-element.27, pred[512,512]{0,1:T(8,128)(4,1)} %copy-done.5, f32[512,2]{0,1:T(2,128)S(1)} %get-tuple-element.12, ...), kind=kOutput, calls=%fused_computation.40 | convolution fusion | flops 137232384 | bytes 3682304 | tf_op jit(solution)/shard_map/hqk,khd->qhd/dot_general | solution.py:51
  65.9 0.0 collective-permute-done.5
  65.9 1.8 copy.60
  67.7 3.4 %fusion.25 = f32[512,2,128]{0,2,1:T(8,128)} fusion(f32[512,2,128]{0,2,1:T(8,128)} %fusion.24, bf16[512,2,128]{0,2,1:T(8,128)(2,1)} %bitcast.212, f32[2,512,512]{1,2,0:T(8,128)} %copy-done.4, f32[2,512]{1,0:T(2,128)S(1)} %get-tuple-element.25, pred[512,512]{0,1:T(8,128)(4,1)S(1)} %get-tuple-element.15, f32[512,2]{0,1:T(2,128)S(1)} %get-tuple-element.10, ...), kind=kOutput, calls=%fused_computation.41 | convolution fusion | flops 137232384 | bytes 3682304 | tf_op jit(solution)/shard_map/hqk,khd->qhd/dot_general | solution.py:51
  71.1 0.0 collective-permute-done.8
  71.1 1.1 copy.65
  72.2 3.3 %fusion.26 = f32[512,2,128]{0,2,1:T(8,128)} fusion(f32[512,2,128]{0,2,1:T(8,128)} %fusion.25, bf16[512,2,128]{0,2,1:T(8,128)(2,1)S(1)} %bitcast.213, f32[2,512,512]{1,2,0:T(8,128)} %copy-done.2, f32[2,512]{1,0:T(2,128)S(1)} %get-tuple-element.23, pred[512,512]{0,1:T(8,128)(4,1)S(1)} %get-tuple-element.16, f32[512,2]{0,1:T(2,128)S(1)} %get-tuple-element.8, ...), kind=kOutput, calls=%fused_computation.42 | convolution fusion | flops 137232384 | bytes 3682304 | tf_op jit(solution)/shard_map/hqk,khd->qhd/dot_general | solution.py:51
  75.5 0.0 collective-permute-done.11
  75.5 1.1 copy.70
  76.6 2.5 %fusion.28 = bf16[512,2,128]{0,2,1:T(8,128)(2,1)S(1)} fusion(f32[512,2,128]{0,2,1:T(8,128)} %fusion.26, bf16[512,2,128]{0,2,1:T(8,128)(2,1)S(1)} %bitcast.210, f32[2,512,512]{1,2,0:T(8,128)} %copy-done.1, f32[2,512]{1,0:T(2,128)S(1)} %get-tuple-element.21, pred[512,512]{0,1:T(8,128)(4,1)S(1)} %get-tuple-element.17, f32[512,2]{0,1:T(2,128)S(1)} %get-tuple-element.5, ...), kind=kOutput, calls=%fused_computation.44 | convolution fusion | flops 137363456 | bytes 3420160 | tf_op jit(solution)/shard_map/hqk,khd->qhd/dot_general | solution.py:51
  79.1 3.9 %convolution_convert_fusion = bf16[512,5120]{1,0:T(8,128)(2,1)} fusion(bf16[512,256]{0,1:T(8,128)(2,1)S(1)} %bitcast.208, bf16[256,5120]{1,0:T(8,128)(2,1)S(1)} %copy-done), kind=kOutput, calls=%fused_computation | convolution fusion | flops 1344798720 | bytes 8126464 | tf_op jit(solution)/shard_map/dot_general | solution.py:92
  83.0 7.9 %copy.72 = bf16[512,5120]{0,1:T(8,128)(2,1)} copy(bf16[512,5120]{1,0:T(8,128)(2,1)} %convolution_convert_fusion) | data formatting | bytes 10485760 | tf_op jit(solution)/shard_map/convert_element_type | solution.py:93
  90.9 5.3 %copy.73 = bf16[4,4,512,320]{2,3,1,0:T(8,128)(2,1)} copy(bf16[4,4,512,320]{2,3,0,1:T(8,128)(2,1)} %bitcast.207) | data formatting | bytes 10485760 | tf_op jit(solution)/shard_map/transpose | solution.py:21
  96.2 0.0 reduce-scatter.3.cloned.1.call-update
  96.3 0.0 reduce-scatter.5.cloned.1.call-start
  96.3 77.9 %reduce-scatter.3.cloned.1.call-done = bf16[4,512,320]{1,2,0:T(8,128)(2,1)} async-done(((bf16[16,512,320]{1,2,0:T(8,128)(2,1)}), bf16[4,512,320]{1,2,0:T(8,128)(2,1)}) %reduce-scatter.3.cloned.1.call-update) | async-done | bytes 1310736 | tf_op jit(solution)/shard_map/reduce_scatter | solution.py:23
  174.2 0.0 reduce-scatter.5.cloned.1.call-update
  174.2 58.8 %reduce-scatter.5.cloned.1.call-done = bf16[1,512,320]{1,2,0:T(8,128)(2,1)} async-done(((bf16[4,512,320]{1,2,0:T(8,128)(2,1)}), bf16[1,512,320]{1,2,0:T(8,128)(2,1)}) %reduce-scatter.5.cloned.1.call-update) | async-done | bytes 327696 | tf_op jit(solution)/shard_map/reduce_scatter | solution.py:23
  (7 shorter events, 0.0 us)
Async XLA Ops:
  6.5 72.5 %copy-start = (bf16[256,5120]{1,0:T(8,128)(2,1)S(1)}, bf16[256,5120]{1,0:T(8,128)(2,1)}, u32[]{:S(2)}) copy-start(bf16[256,5120]{1,0:T(8,128)(2,1)} %param.9) | copy-start | bytes 7864324
  6.5 167.7 %reduce-scatter.3.cloned.1.call-start = ((), (), s32[]{:S(2)}) async-start(), calls=%async_computation.2 | async-start | bytes 6553600 | tf_op jit(solution)/shard_map/reduce_scatter | solution.py:23
  7.4 23.4 %collective-permute-start = (s32[512]{0:T(512)S(1)}, s32[512]{0:T(512)S(1)}, u32[]{:S(2)}, u32[]{:S(2)}) collective-permute-start(s32[512]{0:T(512)S(1)} %broadcast_add_fusion), channel_id=1, source_target_pairs={{0,16},{16,32},{32,48},{48,64},{64,80},{80,96},{96,112},{112,128},... | collective-permute-start | bytes 6152 | tf_op jit(solution)/shard_map/ppermute | solution.py:15
  12.0 21.4 %collective-permute-start.3 = (s32[512]{0:T(512)S(1)}, s32[512]{0:T(512)S(1)}, u32[]{:S(2)}, u32[]{:S(2)}) collective-permute-start(s32[512]{0:T(512)S(1)} %broadcast_add_fusion), channel_id=1, source_target_pairs={{16,0},{32,16},{48,32},{64,48},{80,64},{96,80},{112,96},{128,112},... | collective-permute-start | bytes 6152 | tf_op jit(solution)/shard_map/ppermute | solution.py:15
  21.1 15.0 %collective-permute-start.6 = (s32[512]{0:T(512)S(1)}, s32[512]{0:T(512)S(1)}, u32[]{:S(2)}, u32[]{:S(2)}) collective-permute-start(s32[512]{0:T(512)S(1)} %broadcast_add_fusion), channel_id=1, source_target_pairs={{0,32},{16,48},{32,64},{48,80},{64,96},{80,112},{96,128},{112,144}... | collective-permute-start | bytes 6152 | tf_op jit(solution)/shard_map/ppermute | solution.py:15
  22.4 15.0 %collective-permute-start.9 = (s32[512]{0:T(512)S(1)}, s32[512]{0:T(512)S(1)}, u32[]{:S(2)}, u32[]{:S(2)}) collective-permute-start(s32[512]{0:T(512)S(1)} %broadcast_add_fusion), channel_id=1, source_target_pairs={{32,0},{48,16},{64,32},{80,48},{96,64},{112,80},{128,96},{144,112}... | collective-permute-start | bytes 6152 | tf_op jit(solution)/shard_map/ppermute | solution.py:15
  25.5 18.0 %collective-permute-start.1 = (bf16[512,256]{0,1:T(8,128)(2,1)}, bf16[512,256]{0,1:T(8,128)(2,1)}, u32[]{:S(2)}, u32[]{:S(2)}) collective-permute-start(bf16[512,256]{0,1:T(8,128)(2,1)} %copy.52), channel_id=1, source_target_pairs={{0,16},{16,32},{32,48},{48,64},{64,80},{80,96},{96,112},{112,128},... | collective-permute-start | bytes 786440 | tf_op jit(solution)/shard_map/ppermute | solution.py:15
  30.8 14.6 %copy-start.7 = (bf16[512,256]{1,0:T(8,128)(2,1)S(1)}, bf16[512,256]{1,0:T(8,128)(2,1)}, u32[]{:S(2)}) copy-start(bf16[512,256]{1,0:T(8,128)(2,1)} %param.5) | copy-start | bytes 786436
  30.8 16.2 %collective-permute-start.7 = (bf16[512,256]{0,1:T(8,128)(2,1)}, bf16[512,256]{0,1:T(8,128)(2,1)S(1)}, u32[]{:S(2)}, u32[]{:S(2)}) collective-permute-start(bf16[512,256]{0,1:T(8,128)(2,1)} %copy.52), channel_id=1, source_target_pairs={{0,32},{16,48},{32,64},{48,80},{64,96},{80,112},{96,128},{112,144}... | collective-permute-start | bytes 786440 | tf_op jit(solution)/shard_map/ppermute | solution.py:15
  33.3 18.7 %collective-permute-start.4 = (bf16[512,256]{0,1:T(8,128)(2,1)}, bf16[512,256]{0,1:T(8,128)(2,1)S(1)}, u32[]{:S(2)}, u32[]{:S(2)}) collective-permute-start(bf16[512,256]{0,1:T(8,128)(2,1)} %copy.52), channel_id=1, source_target_pairs={{16,0},{32,16},{48,32},{64,48},{80,64},{96,80},{112,96},{128,112},... | collective-permute-start | bytes 786440 | tf_op jit(solution)/shard_map/ppermute | solution.py:15
  36.0 18.1 %collective-permute-start.10 = (bf16[512,256]{0,1:T(8,128)(2,1)}, bf16[512,256]{0,1:T(8,128)(2,1)S(1)}, u32[]{:S(2)}, u32[]{:S(2)}) collective-permute-start(bf16[512,256]{0,1:T(8,128)(2,1)} %copy.52), channel_id=1, source_target_pairs={{32,0},{48,16},{64,32},{80,48},{96,64},{112,80},{128,96},{144,112}... | collective-permute-start | bytes 786440 | tf_op jit(solution)/shard_map/ppermute | solution.py:15
  37.3 23.3 %collective-permute-start.2 = (bf16[512,256]{1,0:T(8,128)(2,1)}, bf16[512,256]{1,0:T(8,128)(2,1)}, u32[]{:S(2)}, u32[]{:S(2)}) collective-permute-start(bf16[512,256]{1,0:T(8,128)(2,1)} %param.7), channel_id=1, source_target_pairs={{0,16},{16,32},{32,48},{48,64},{64,80},{80,96},{96,112},{112,128},... | collective-permute-start | bytes 786440 | tf_op jit(solution)/shard_map/ppermute | solution.py:15
  41.8 14.9 %copy-start.5 = (pred[512,512]{0,1:T(8,128)(4,1)}, pred[512,512]{0,1:T(8,128)(4,1)S(1)}, u32[]{:S(2)}) copy-start(pred[512,512]{0,1:T(8,128)(4,1)S(1)} %get-tuple-element.14) | copy-start | bytes 786436
  43.5 22.4 %collective-permute-start.5 = (bf16[512,256]{1,0:T(8,128)(2,1)}, bf16[512,256]{1,0:T(8,128)(2,1)}, u32[]{:S(2)}, u32[]{:S(2)}) collective-permute-start(bf16[512,256]{1,0:T(8,128)(2,1)} %param.7), channel_id=1, source_target_pairs={{16,0},{32,16},{48,32},{64,48},{80,64},{96,80},{112,96},{128,112},... | collective-permute-start | bytes 786440 | tf_op jit(solution)/shard_map/ppermute | solution.py:15
  47.0 9.7 %copy-start.3 = (f32[2,512,512]{1,2,0:T(8,128)}, f32[2,512,512]{1,2,0:T(8,128)S(1)}, u32[]{:S(2)}) copy-start(f32[2,512,512]{1,2,0:T(8,128)S(1)} %get-tuple-element.28) | copy-start | bytes 6291460
  47.0 24.1 %collective-permute-start.8 = (bf16[512,256]{1,0:T(8,128)(2,1)}, bf16[512,256]{1,0:T(8,128)(2,1)}, u32[]{:S(2)}, u32[]{:S(2)}) collective-permute-start(bf16[512,256]{1,0:T(8,128)(2,1)} %param.7), channel_id=1, source_target_pairs={{0,32},{16,48},{32,64},{48,80},{64,96},{80,112},{96,128},{112,144}... | collective-permute-start | bytes 786440 | tf_op jit(solution)/shard_map/ppermute | solution.py:15
  52.0 5.8 %copy-start.2 = (f32[2,512,512]{1,2,0:T(8,128)}, f32[2,512,512]{1,2,0:T(8,128)S(1)}, u32[]{:S(2)}) copy-start(f32[2,512,512]{1,2,0:T(8,128)S(1)} %get-tuple-element.24) | copy-start | bytes 6291460
  52.0 23.5 %collective-permute-start.11 = (bf16[512,256]{1,0:T(8,128)(2,1)}, bf16[512,256]{1,0:T(8,128)(2,1)}, u32[]{:S(2)}, u32[]{:S(2)}) collective-permute-start(bf16[512,256]{1,0:T(8,128)(2,1)} %param.7), channel_id=1, source_target_pairs={{32,0},{48,16},{64,32},{80,48},{96,64},{112,80},{128,96},{144,112}... | collective-permute-start | bytes 786440 | tf_op jit(solution)/shard_map/ppermute | solution.py:15
  54.1 3.7 %copy-start.4 = (f32[2,512,512]{1,2,0:T(8,128)}, f32[2,512,512]{1,2,0:T(8,128)S(1)}, u32[]{:S(2)}) copy-start(f32[2,512,512]{1,2,0:T(8,128)S(1)} %get-tuple-element.26) | copy-start | bytes 6291460
  54.8 1.3 copy-start.1
  57.8 1.2 copy-start.6
  96.3 136.8 %reduce-scatter.5.cloned.1.call-start = ((), (), s32[]{:S(2)}) async-start(), calls=%async_computation.3 | async-start | bytes 1638400 | tf_op jit(solution)/shard_map/reduce_scatter | solution.py:23
Sparse Core Ops, SparseCore 0:
  96.4 77.7 reduce-scatter.2
  177.3 55.6 reduce-scatter.4
where the time goes:
time: 241 us; the launch traced here: 240 us
  waiting for transfers between devices  137 us (57%)
  starting transfers between devices  37.6 us (16%)
  local copies, waits for them, and re-layouts  23.9 us (10%)
  matrix products  23.3 us (10%)
  between operations  13.7 us (6%)
  other arithmetic  4.55 us (2%)
    reduce_scatter x2, waiting for transfers between devices, reduced_to_own(): pieces = lax.psum_scatter(pieces, axes[k], scatter_dimension=0, tiled=True)  137 us
    ppermute x12, starting transfers between devices, shifted(): return lax.ppermute(block, axis, route)  37.5 us
    dot_general x5, matrix products, attend(): jnp.einsum('hqk,khd->qhd', weights.astype(jnp.bfloat16), value_heads, pre...  14.3 us
    convert_element_type x1, local copies, waits for them, and re-layouts, shards(): term.astype(jnp.bfloat16)  7.95 us
    ppermute x4, local copies, waits for them, and re-layouts, shifted(): return lax.ppermute(block, axis, route)  5.77 us
    transpose x1, local copies, waits for them, and re-layouts, reduced_to_own(): jnp.moveaxis(pieces, sequence, range(len(axes))).reshape(-1, *inside)  5.3 us
    dot_general x5, matrix products, attend(): jnp.einsum('qhd,khd->hqk', query_heads, key_heads, preferred_element_type...  5.16 us
  transfers between devices with their start and end apart: 14, of which 2 were waited for; matrix products, arithmetic and copies ran while one was open for 12% of the time, Pallas kernels for 0%

commit v1 on v0

v1 whole, which is shorter than its diff:
```python
import functools
import math

import jax
import jax.numpy as jnp
from jax import lax
from jax.experimental import pallas as pl
from jax.experimental.pallas import tpu as pltpu
from jax.sharding import Mesh
from jax.sharding import PartitionSpec as P

Y = 8
ZH = 4
HD = 128
CH = 4
NEG = -1e30
MESH = pl.DeviceIdType.MESH
NEAR, FAR, PARTNER, RELAY, OWN = range(5)
IDS = 4


def tile_lanes(x, n):
    return jnp.concatenate([x] * n, axis=1)


def kernel(
    yn, xn, q_hbm, k_hbm, v_hbm, ids_hbm, w_hbm, out_ref,
    qv, kv, idr, qid, m_sc, l_sc, acc_sc, ag, wg, wrelay, xs, xr,
    kv_s, kv_r, wz_s, wz_r, wp_s, wp_r, wm_s, wm_r, wq_s, wq_r, az_s, az_r, x_s, x_r, loc,
):
    rows = q_hbm.shape[0]
    tr = rows // CH
    half = tr // 2
    slab = w_hbm.shape[2] // ZH
    own = out_ref.shape[1]
    win = xs.shape[3]
    factor = HD ** -0.5 * math.log2(math.e)

    s_at = lax.axis_index("seq")
    z_at = lax.axis_index("zh")
    x_at = lax.axis_index("x")
    sn = lax.axis_size("seq")
    core = lax.rem(s_at, 2)
    sgn = 2 * core - 1
    near = lax.rem(s_at + sgn + sn, sn)
    far_to = lax.rem(s_at - 2 * sgn + sn, sn)
    far_from = lax.rem(s_at + 2 * sgn + sn, sn)
    partner = s_at - sgn
    y_at = lax.rem(s_at // 2, yn)
    line = (s_at // (2 * yn)) * (2 * yn)
    y_up = line + lax.rem(y_at + 1, yn) * 2 + core
    y_down = line + lax.rem(y_at + yn - 1, yn) * 2 + core
    z_up = lax.rem(z_at + 1, ZH)
    z_two = lax.rem(z_at + 2, ZH)
    z_down = lax.rem(z_at + ZH - 1, ZH)

    def wblock(distance):
        return lax.rem(y_at + distance + 2 * yn, yn) * 2 + core

    me_block = 2 * y_at + core

    def remote(src, dst, send, recv, device):
        return pltpu.make_async_remote_copy(
            src_ref=src, dst_ref=dst, send_sem=send, recv_sem=recv,
            device_id=device, device_id_type=MESH,
        )

    sent = []

    def go(copy):
        copy.start()
        sent.append(copy)

    def piece_src(p):
        if p == IDS:
            return ids_hbm
        src = k_hbm if p % 2 == 0 else v_hbm
        return src.at[:, pl.ds((p // 2) * HD, HD)]

    def piece_dst(p, slot):
        return idr.at[slot] if p == IDS else kv.at[slot, p]

    targets = {NEAR: {"seq": near}, FAR: {"seq": far_to}, PARTNER: {"seq": partner}, RELAY: {"seq": partner}}

    def piece(p, slot):
        src = piece_dst(p, NEAR) if slot == RELAY else piece_src(p)
        return remote(src, piece_dst(p, slot), kv_s.at[p, slot], kv_r.at[p, slot], targets[slot])

    def cols(z):
        return pl.ds(pl.multiple_of(z * slab, 128), slab)

    local = [pltpu.make_async_copy(piece_src(p), piece_dst(p, OWN), loc.at[p]) for p in range(5)]
    local.append(pltpu.make_async_copy(q_hbm, qv, loc.at[5]))
    w_local = pltpu.make_async_copy(w_hbm.at[:, :, cols(z_at)], wg.at[:, 0], loc.at[6])
    for copy in local:
        copy.start()
    w_local.start()

    barrier = pltpu.get_barrier_semaphore()
    peers = [{"seq": near}, {"seq": partner}, {"seq": far_to}, {"seq": far_from}, {"seq": y_up}, {"seq": y_down},
             {"zh": z_up}, {"zh": z_down}]
    peers += [{"x": lax.rem(x_at + r, xn)} for r in range(1, xn)]
    for peer in peers:
        pl.semaphore_signal(barrier, inc=1, device_id=peer, device_id_type=MESH)
    pl.semaphore_wait(barrier, len(peers))

    for p in (IDS, 0, 1):
        for slot in (NEAR, FAR, PARTNER):
            go(piece(p, slot))
    wz = [
        remote(w_hbm.at[me_block, :, cols(z_two)], wrelay, wz_s.at[0], wz_r.at[0], {"zh": z_up}),
        remote(w_hbm.at[me_block, :, cols(z_up)], wg.at[me_block, 1], wz_s.at[1], wz_r.at[1], {"zh": z_up}),
        remote(w_hbm.at[me_block, :, cols(z_down)], wg.at[me_block, 3], wz_s.at[2], wz_r.at[2], {"zh": z_down}),
        remote(wrelay, wg.at[me_block, 2], wz_s.at[3], wz_r.at[3], {"zh": z_up}),
    ]
    for copy in wz[:3]:
        go(copy)
    for p in (2, 3):
        for slot in (NEAR, FAR, PARTNER):
            go(piece(p, slot))

    for copy in local:
        copy.wait()
    for i in range(rows // 128):
        wide = jnp.broadcast_to(idr[OWN, 0:1, i * 128:(i + 1) * 128].astype(jnp.float32), (128, 128))
        qid[i * 128:(i + 1) * 128, :] = jnp.transpose(wide)

    def attn(slot, head, first=False):
        def body(t, carry):
            at = pl.ds(pl.multiple_of(t * tr, tr), tr)
            q = qv[at, head * HD:(head + 1) * HD]
            scores = lax.dot_general(
                q, kv[slot, 2 * head], (((1,), (1,)), ((), ())), preferred_element_type=jnp.float32
            )
            n = rows // HD
            mine = tile_lanes(qid[at, :], n)
            theirs = jnp.broadcast_to(idr[slot, 0:1, :].astype(jnp.float32), (tr, rows))
            scores = jnp.where(mine == theirs, scores, NEG)
            top = jnp.broadcast_to(jnp.max(scores, axis=1, keepdims=True), (tr, HD))
            if not first:
                old = m_sc[at, :]
                top = jnp.maximum(old, top)
            weights = jnp.exp2((scores - tile_lanes(top, n)) * factor)
            part = weights[:, :HD]
            for i in range(1, n):
                part = part + weights[:, i * HD:(i + 1) * HD]
            summed = jnp.dot(weights.astype(jnp.bfloat16), kv[slot, 2 * head + 1], preferred_element_type=jnp.float32)
            if not first:
                scale = jnp.exp2((old - top) * factor)
                part = part + l_sc[at, :] * scale
                summed = summed + acc_sc[at, :] * scale
            m_sc[at, :] = top
            l_sc[at, :] = part
            acc_sc[at, :] = summed
            return carry

        lax.fori_loop(0, CH, body, 0)

    def finish(head, chunk):
        at = pl.ds(chunk * tr, tr)
        total = jnp.sum(l_sc[at, :], axis=1, keepdims=True)
        ag[0, head, at, :] = (acc_sc[at, :] / total).astype(jnp.bfloat16)

    def az(head, chunk, kind):
        at = pl.ds(chunk * tr, tr)
        low, high = pl.ds(chunk * tr, half), pl.ds(chunk * tr + half, half)
        src, dst, to = [
            (ag.at[0, head, at], ag.at[1, head, at], z_up),
            (ag.at[0, head, at], ag.at[3, head, at], z_down),
            (ag.at[1, head, low], ag.at[2, head, low], z_up),
            (ag.at[3, head, high], ag.at[2, head, high], z_down),
        ][kind]
        return remote(src, dst, az_s.at[head, chunk, kind], az_r.at[head, chunk, kind], {"zh": to})

    def z_relay(head, chunk):
        for kind in (0, 1):
            az(head, chunk, kind).wait_recv()
            go(az(head, chunk, kind + 2))

    ups, downs = yn // 2, (yn - 1) // 2

    def w_step(kind, t):
        if kind == "up":
            src, sems, to = wblock(-t), (wp_s.at[t], wp_r.at[t]), y_up
        elif kind == "down":
            src, sems, to = wblock(t), (wm_s.at[t], wm_r.at[t]), y_down
        else:
            src, sems, to = wblock(t), (wq_s.at[t % yn], wq_r.at[t % yn]), partner
        block = wg.at[src, pl.ds(1, ZH - 1)]
        return remote(block, block, *sems, {"seq": to})

    def w_advance(t):
        w_step("up", t).wait_recv()
        if t + 1 < ups:
            go(w_step("up", t + 1))
        go(w_step("partner", -1 - t))
        if t < downs:
            w_step("down", t).wait_recv()
            if t + 1 < downs:
                go(w_step("down", t + 1))
            go(w_step("partner", 1 + t))

    def arrive(slot, *pieces):
        for p in pieces:
            piece(p, slot).wait_recv()
            if slot == NEAR:
                go(piece(p, RELAY))

    attn(OWN, 0, first=True)
    arrive(PARTNER, IDS, 0, 1)
    attn(PARTNER, 0)
    arrive(NEAR, IDS, 0, 1)
    attn(NEAR, 0)
    wz[0].wait_recv()
    go(wz[3])
    arrive(FAR, IDS, 0, 1)
    attn(FAR, 0)
    arrive(RELAY, IDS, 0, 1)
    attn(RELAY, 0)
    for c in range(CH):
        finish(0, c)
        go(az(0, c, 0))
        go(az(0, c, 1))

    arrive(NEAR, 2, 3)
    attn(OWN, 1, first=True)
    for copy in wz[1:]:
        copy.wait_recv()
    go(w_step("up", 0))
    go(w_step("down", 0))
    go(w_step("partner", 0))
    arrive(PARTNER, 2, 3)
    attn(PARTNER, 1)
    attn(NEAR, 1)
    z_relay(0, 0)
    arrive(FAR, 2, 3)
    attn(FAR, 1)
    z_relay(0, 1)
    arrive(RELAY, 2, 3)
    attn(RELAY, 1)
    for c in range(CH):
        finish(1, c)
        go(az(1, c, 0))
        go(az(1, c, 1))
        if c == 1:
            z_relay(0, 2)
        if c == 2:
            z_relay(0, 3)
    for t in range(max(ups, CH)):
        if t < ups:
            w_advance(t)
        if t < CH:
            z_relay(1, t)
    w_local.wait()
    for t in range(yn):
        w_step("partner", t).wait_recv()

    def project(c):
        at = pl.ds(c * tr, tr)
        for head in range(2):
            for kind in (2, 3):
                az(head, c, kind).wait_recv()
        total = None
        for head in range(2):
            left = jnp.concatenate([ag[r, head, at, :] for r in range(ZH)], axis=1)
            n = wg.shape[0] // 2
            right = jnp.concatenate(
                [wg[head * n:(head + 1) * n, r].reshape(HD, slab) for r in range(ZH)], axis=0
            )
            term = jnp.dot(left, right, preferred_element_type=jnp.float32)
            total = term if total is None else total + term
        total = total.astype(jnp.bfloat16)
        for x in range(xn):
            start = (x * own // HD) * HD
            xs[c, x] = total[:, start:start + win]

    def x_copy(c, r):
        to = lax.rem(x_at + r, xn)
        return remote(xs.at[c, to], xr.at[c, r - 1], x_s.at[c, r - 1], x_r.at[c, r - 1], {"x": to})

    for c in range(CH):
        project(c)
        for r in range(1, xn):
            go(x_copy(c, r))

    odd = lax.rem(x_at, 2) == 1
    for c in range(CH):
        total = xs[c, x_at].astype(jnp.float32)
        for r in range(1, xn):
            x_copy(c, r).wait_recv()
            total = total + xr[c, r - 1].astype(jnp.float32)
        mixed = jnp.where(odd, total[:, win - own:], total[:, :own])
        out_ref[c * tr:(c + 1) * tr, :] = mixed.astype(jnp.bfloat16)
    for copy in sent:
        copy.wait_send()


def shards(yn, xn, queries, keys, values, segment_ids, out_weight):
    rows = queries.shape[0]
    depth, features = out_weight.shape
    own = features // (ZH * xn)
    win = -(-own // HD) * HD
    slab = features // ZH
    wb = depth // (2 * yn)
    ids = jnp.broadcast_to(segment_ids[None, :], (8, rows))
    weight = out_weight.reshape(2 * yn, wb, features)
    dma = pltpu.SemaphoreType.DMA
    bf16, f32 = jnp.bfloat16, jnp.float32
    hbm = pl.BlockSpec(memory_space=pl.ANY)
    ups, downs = yn // 2, max(1, (yn - 1) // 2)
    return pl.pallas_call(
        functools.partial(kernel, yn, xn),
        out_shape=jax.ShapeDtypeStruct((rows, own), bf16),
        in_specs=[hbm] * 5,
        out_specs=pl.BlockSpec(memory_space=pltpu.VMEM),
        scratch_shapes=[
            pltpu.VMEM((rows, 2 * HD), bf16),
            pltpu.VMEM((5, 4, rows, HD), bf16),
            pltpu.VMEM((5, 8, rows), jnp.int32),
            pltpu.VMEM((rows, HD), f32),
            pltpu.VMEM((rows, HD), f32),
            pltpu.VMEM((rows, HD), f32),
            pltpu.VMEM((rows, HD), f32),
            pltpu.VMEM((ZH, 2, rows, HD), bf16),
            pltpu.VMEM((2 * yn, ZH, wb, slab), bf16),
            pltpu.VMEM((wb, slab), bf16),
            pltpu.VMEM((CH, xn, rows // CH, win), bf16),
            pltpu.VMEM((CH, xn - 1, rows // CH, win), bf16),
            dma((5, 4)), dma((5, 4)),
            dma((4,)), dma((4,)),
            dma((ups,)), dma((ups,)),
            dma((downs,)), dma((downs,)),
            dma((yn,)), dma((yn,)),
            dma((2, CH, 4)), dma((2, CH, 4)),
            dma((CH, xn - 1)), dma((CH, xn - 1)),
            dma((7,)),
        ],
        compiler_params=pltpu.CompilerParams(
            collective_id=0, has_side_effects=True, vmem_limit_bytes=60 * 1024 * 1024
        ),
    )(queries, keys, values, ids, weight)


def build(mesh, yn):
    sn, hn = mesh.shape["seq"], mesh.shape["head"]
    torus = Mesh(mesh.devices.reshape(sn, ZH, hn // ZH), ("seq", "zh", "x"))
    head = ("zh", "x")
    in_specs = (P("seq", head), P("seq", head), P("seq", head), P("seq"), P(head, None))
    return jax.shard_map(
        functools.partial(shards, yn, hn // ZH),
        mesh=torus, in_specs=in_specs, out_specs=P("seq", head), check_vma=False,
    )


def solution(mesh):
    return build(mesh, Y)
```

time: 241 us -> 95.6 us (0.40)
  the two profiles are of different devices: /device:TPU:1 before, /device:TPU:73 now
where the time goes in v1:
time: 95.6 us; the launch traced here: 95.4 us
  Pallas kernels  92.3 us (97%)
  local copies, waits for them, and re-layouts  3.16 us (3%)
    pallas_call x1, Pallas kernels, shards(): pl.pallas_call(functools.partial(kernel, yn, xn), out_shape=jax.ShapeDtyp...  92.3 us

profile of v1, /device:TPU:73, one launch (start us, length us, event | category | flops | bytes accessed | tf_op | source)
XLA Modules:
  0.0 95.4 jit_solution(15196144494980010769)
XLA Ops:
  0.0 1.3 %broadcast_in_dim.2.ids_hbm = s32[8,512]{1,0:T(8,128)} broadcast(s32[512]{0:T(512)} %param.8), dimensions={1} | broadcast | bytes 18432 | tf_op jit(solution)/shard_map/broadcast_in_dim | solution.py:305
  1.3 92.3 %shard_map.55 = bf16[512,320]{1,0:T(8,128)(2,1)} custom-call(bf16[512,256]{1,0:T(8,128)(2,1)} %q_hbm.1, bf16[512,256]{1,0:T(8,128)(2,1)} %k_hbm.1, bf16[512,256]{1,0:T(8,128)(2,1)} %v_hbm.1, s32[8,512]{1,0:T(8,128)} %broadcast_in_dim.2.ids_hbm, bf16[16,16,5120]{2,1,0:T(8,128)(2,1)} %bitcast.1), custom_call_target="tpu_custom_call" | custom-call | tf_op jit(solution)/shard_map/pallas_call | solution.py:311
  93.6 1.9 %copy.6 = bf16[512,320]{0,1:T(8,128)(2,1)} copy(bf16[512,320]{1,0:T(8,128)(2,1)} %shard_map.55) | data formatting | bytes 655360 | tf_op jit(solution)/shard_map/pallas_call | solution.py:311

commit v2 on v1

--- a/solution.py
+++ b/solution.py
@@ -24,15 +24,15 @@
 
 
 def kernel(
-    yn, xn, q_hbm, k_hbm, v_hbm, ids_hbm, w_hbm, out_ref,
-    qv, kv, idr, qid, m_sc, l_sc, acc_sc, ag, wg, wrelay, xs, xr,
-    kv_s, kv_r, wz_s, wz_r, wp_s, wp_r, wm_s, wm_r, wq_s, wq_r, az_s, az_r, x_s, x_r, loc,
+    yn, xn, q_hbm, k_hbm, v_hbm, ids_hbm, w_hbm, out_hbm,
+    qv, kv, idr, qid, m_sc, l_sc, acc_sc, ag, wg, wrelay, xs, xr, ot,
+    kv_s, kv_r, wz_s, wz_r, wp_s, wp_r, wm_s, wm_r, wq_s, wq_r, az_s, az_r, x_s, x_r, o_s, loc,
 ):
     rows = q_hbm.shape[0]
     tr = rows // CH
     half = tr // 2
     slab = w_hbm.shape[2] // ZH
-    own = out_ref.shape[1]
+    own = out_hbm.shape[0]
     win = xs.shape[3]
     factor = HD ** -0.5 * math.log2(math.e)
 
@@ -154,7 +154,7 @@
             acc_sc[at, :] = summed
             return carry
 
-        lax.fori_loop(0, CH, body, 0)
+        lax.fori_loop(0, CH, body, 0, unroll=True)
 
     def finish(head, chunk):
         at = pl.ds(chunk * tr, tr)
@@ -177,6 +177,10 @@
             az(head, chunk, kind).wait_recv()
             go(az(head, chunk, kind + 2))
 
+    def z_direct(head, chunk):
+        go(az(head, chunk, 0))
+        go(az(head, chunk, 1))
+
     ups, downs = yn // 2, (yn - 1) // 2
 
     def w_step(kind, t):
@@ -190,6 +194,8 @@
         return remote(block, block, *sems, {"seq": to})
 
     def w_advance(t):
+        if t >= ups:
+            return
         w_step("up", t).wait_recv()
         if t + 1 < ups:
             go(w_step("up", t + 1))
@@ -209,48 +215,46 @@
     attn(OWN, 0, first=True)
     arrive(PARTNER, IDS, 0, 1)
     attn(PARTNER, 0)
+    wz[0].wait_recv()
+    go(wz[3])
     arrive(NEAR, IDS, 0, 1)
     attn(NEAR, 0)
-    wz[0].wait_recv()
-    go(wz[3])
     arrive(FAR, IDS, 0, 1)
     attn(FAR, 0)
     arrive(RELAY, IDS, 0, 1)
     attn(RELAY, 0)
     for c in range(CH):
         finish(0, c)
-        go(az(0, c, 0))
-        go(az(0, c, 1))
-
-    arrive(NEAR, 2, 3)
-    attn(OWN, 1, first=True)
+        z_direct(0, c)
+
     for copy in wz[1:]:
         copy.wait_recv()
     go(w_step("up", 0))
     go(w_step("down", 0))
     go(w_step("partner", 0))
+    arrive(NEAR, 2, 3)
+    attn(OWN, 1, first=True)
     arrive(PARTNER, 2, 3)
     attn(PARTNER, 1)
+    z_relay(0, 0)
     attn(NEAR, 1)
-    z_relay(0, 0)
+    z_relay(0, 1)
     arrive(FAR, 2, 3)
     attn(FAR, 1)
-    z_relay(0, 1)
+    w_advance(0)
     arrive(RELAY, 2, 3)
     attn(RELAY, 1)
     for c in range(CH):
         finish(1, c)
-        go(az(1, c, 0))
-        go(az(1, c, 1))
-        if c == 1:
-            z_relay(0, 2)
-        if c == 2:
-            z_relay(0, 3)
-    for t in range(max(ups, CH)):
-        if t < ups:
-            w_advance(t)
-        if t < CH:
-            z_relay(1, t)
+        if c < 2:
+            z_direct(1, c)
+    z_relay(0, 2)
+    w_advance(1)
+    z_relay(0, 3)
+    for t in range(2, max(ups, 4)):
+        w_advance(t)
+        z_relay(1, t - 2)
+        z_direct(1, t)
     w_local.wait()
     for t in range(yn):
         w_step("partner", t).wait_recv()
@@ -273,26 +277,42 @@
         for x in range(xn):
             start = (x * own // HD) * HD
             xs[c, x] = total[:, start:start + win]
+        for r in range(1, xn):
+            go(x_copy(c, r))
 
     def x_copy(c, r):
         to = lax.rem(x_at + r, xn)
         return remote(xs.at[c, to], xr.at[c, r - 1], x_s.at[c, r - 1], x_r.at[c, r - 1], {"x": to})
 
-    for c in range(CH):
-        project(c)
-        for r in range(1, xn):
-            go(x_copy(c, r))
-
     odd = lax.rem(x_at, 2) == 1
-    for c in range(CH):
+
+    def out_copy(c):
+        return pltpu.make_async_copy(ot.at[c], out_hbm.at[:, pl.ds(c * tr, tr)], o_s.at[c])
+
+    def mix(c):
         total = xs[c, x_at].astype(jnp.float32)
         for r in range(1, xn):
             x_copy(c, r).wait_recv()
             total = total + xr[c, r - 1].astype(jnp.float32)
-        mixed = jnp.where(odd, total[:, win - own:], total[:, :own])
-        out_ref[c * tr:(c + 1) * tr, :] = mixed.astype(jnp.bfloat16)
+        total = jnp.transpose(total)
+        mixed = jnp.where(odd, total[win - own:], total[:own])
+        ot[c] = mixed.astype(jnp.bfloat16)
+        out_copy(c).start()
+
+    project(0)
+    z_relay(1, 2)
+    project(1)
+    z_relay(1, 3)
+    mix(0)
+    project(2)
+    mix(1)
+    project(3)
+    mix(2)
+    mix(3)
     for copy in sent:
         copy.wait_send()
+    for c in range(CH):
+        out_copy(c).wait()
 
 
 def shards(yn, xn, queries, keys, values, segment_ids, out_weight):
@@ -302,21 +322,21 @@
     win = -(-own // HD) * HD
     slab = features // ZH
     wb = depth // (2 * yn)
-    ids = jnp.broadcast_to(segment_ids[None, :], (8, rows))
+    ids = segment_ids.reshape(1, rows)
     weight = out_weight.reshape(2 * yn, wb, features)
     dma = pltpu.SemaphoreType.DMA
     bf16, f32 = jnp.bfloat16, jnp.float32
     hbm = pl.BlockSpec(memory_space=pl.ANY)
     ups, downs = yn // 2, max(1, (yn - 1) // 2)
-    return pl.pallas_call(
+    out = pl.pallas_call(
         functools.partial(kernel, yn, xn),
-        out_shape=jax.ShapeDtypeStruct((rows, own), bf16),
+        out_shape=jax.ShapeDtypeStruct((own, rows), bf16),
         in_specs=[hbm] * 5,
-        out_specs=pl.BlockSpec(memory_space=pltpu.VMEM),
+        out_specs=hbm,
         scratch_shapes=[
             pltpu.VMEM((rows, 2 * HD), bf16),
             pltpu.VMEM((5, 4, rows, HD), bf16),
-            pltpu.VMEM((5, 8, rows), jnp.int32),
+            pltpu.VMEM((5, 1, rows), jnp.int32),
             pltpu.VMEM((rows, HD), f32),
             pltpu.VMEM((rows, HD), f32),
             pltpu.VMEM((rows, HD), f32),
@@ -326,6 +346,7 @@
             pltpu.VMEM((wb, slab), bf16),
             pltpu.VMEM((CH, xn, rows // CH, win), bf16),
             pltpu.VMEM((CH, xn - 1, rows // CH, win), bf16),
+            pltpu.VMEM((CH, own, rows // CH), bf16),
             dma((5, 4)), dma((5, 4)),
             dma((4,)), dma((4,)),
             dma((ups,)), dma((ups,)),
@@ -333,12 +354,13 @@
             dma((yn,)), dma((yn,)),
             dma((2, CH, 4)), dma((2, CH, 4)),
             dma((CH, xn - 1)), dma((CH, xn - 1)),
-            dma((7,)),
+            dma((CH,)), dma((7,)),
         ],
         compiler_params=pltpu.CompilerParams(
             collective_id=0, has_side_effects=True, vmem_limit_bytes=60 * 1024 * 1024
         ),
     )(queries, keys, values, ids, weight)
+    return jnp.transpose(out)
 
 
 def build(mesh, yn):

time: 95.6 us -> 87.1 us (0.911)
  the two profiles are of different devices: /device:TPU:73 before, /device:TPU:80 now
where the time goes in v2:
time: 87.1 us; the launch traced here: 87 us
  Pallas kernels  85.3 us (98%)
  local copies, waits for them, and re-layouts  1.72 us (2%)
    pallas_call x1, Pallas kernels, shards(): pl.pallas_call(functools.partial(kernel, yn, xn), out_shape=jax.ShapeDtyp...  85.3 us

profile of v2, /device:TPU:80, one launch (start us, length us, event | category | flops | bytes accessed | tf_op | source)
XLA Modules:
  0.0 87.0 jit_solution(14718004859373706904)
XLA Ops:
  0.0 85.3 %shard_map.55 = bf16[320,512]{1,0:T(8,128)(2,1)} custom-call(bf16[512,256]{1,0:T(8,128)(2,1)} %q_hbm.1, bf16[512,256]{1,0:T(8,128)(2,1)} %k_hbm.1, bf16[512,256]{1,0:T(8,128)(2,1)} %v_hbm.1, s32[1,512]{1,0:T(1,128)} %bitcast.5, bf16[16,16,5120]{2,1,0:T(8,128)(2,1)} %bitcast.3), custom_call_target="tpu_custom_call" | custom-call | tf_op jit(solution)/shard_map/pallas_call | solution.py:331
  85.3 1.7 %copy.7 = bf16[512,320]{0,1:T(8,128)(2,1)} copy(bf16[512,320]{0,1:T(8,128)(2,1)} %bitcast.4) | data formatting | bytes 655360

commit v3 on v2

--- a/solution.py
+++ b/solution.py
@@ -30,10 +30,8 @@
 ):
     rows = q_hbm.shape[0]
     tr = rows // CH
-    half = tr // 2
     slab = w_hbm.shape[2] // ZH
     own = out_hbm.shape[0]
-    win = xs.shape[3]
     factor = HD ** -0.5 * math.log2(math.e)
 
     s_at = lax.axis_index("seq")
@@ -67,9 +65,18 @@
 
     sent = []
 
-    def go(copy):
-        copy.start()
-        sent.append(copy)
+    outer = jnp.logical_and(s_at + sgn >= 0, s_at + sgn < sn)
+    inner = jnp.logical_and(s_at - 2 * sgn >= 0, s_at - 2 * sgn < sn)
+
+    def where(condition, act):
+        if condition is None:
+            act()
+        else:
+            pl.when(condition)(act)
+
+    def go(copy, condition=None):
+        where(condition, copy.start)
+        sent.append((copy, condition))
 
     def piece_src(p):
         if p == IDS:
@@ -81,6 +88,9 @@
         return idr.at[slot] if p == IDS else kv.at[slot, p]
 
     targets = {NEAR: {"seq": near}, FAR: {"seq": far_to}, PARTNER: {"seq": partner}, RELAY: {"seq": partner}}
+
+    gives = {NEAR: outer, FAR: inner, PARTNER: None, RELAY: outer}
+    gets = {NEAR: outer, FAR: outer, PARTNER: None, RELAY: inner, OWN: None}
 
     def piece(p, slot):
         src = piece_dst(p, NEAR) if slot == RELAY else piece_src(p)
@@ -104,20 +114,23 @@
         pl.semaphore_signal(barrier, inc=1, device_id=peer, device_id_type=MESH)
     pl.semaphore_wait(barrier, len(peers))
 
-    for p in (IDS, 0, 1):
-        for slot in (NEAR, FAR, PARTNER):
-            go(piece(p, slot))
+    by = jnp.where(core == 0, z_up, z_down)
     wz = [
-        remote(w_hbm.at[me_block, :, cols(z_two)], wrelay, wz_s.at[0], wz_r.at[0], {"zh": z_up}),
+        remote(w_hbm.at[me_block, :, cols(z_two)], wrelay, wz_s.at[0], wz_r.at[0], {"zh": by}),
         remote(w_hbm.at[me_block, :, cols(z_up)], wg.at[me_block, 1], wz_s.at[1], wz_r.at[1], {"zh": z_up}),
         remote(w_hbm.at[me_block, :, cols(z_down)], wg.at[me_block, 3], wz_s.at[2], wz_r.at[2], {"zh": z_down}),
-        remote(wrelay, wg.at[me_block, 2], wz_s.at[3], wz_r.at[3], {"zh": z_up}),
+        remote(wrelay, wg.at[me_block, 2], wz_s.at[3], wz_r.at[3], {"zh": by}),
     ]
-    for copy in wz[:3]:
-        go(copy)
-    for p in (2, 3):
-        for slot in (NEAR, FAR, PARTNER):
-            go(piece(p, slot))
+
+    def send_pieces(*pieces):
+        for p in pieces:
+            for slot in (NEAR, FAR, PARTNER):
+                go(piece(p, slot), gives[slot])
+
+    go(wz[0])
+    send_pieces(IDS, 0, 1)
+    go(wz[1])
+    go(wz[2])
 
     for copy in local:
         copy.wait()
@@ -154,28 +167,38 @@
             acc_sc[at, :] = summed
             return carry
 
-        lax.fori_loop(0, CH, body, 0, unroll=True)
+        def run():
+            lax.fori_loop(0, CH, body, 0, unroll=True)
+
+        where(gets[slot], run)
 
     def finish(head, chunk):
         at = pl.ds(chunk * tr, tr)
         total = jnp.sum(l_sc[at, :], axis=1, keepdims=True)
         ag[0, head, at, :] = (acc_sc[at, :] / total).astype(jnp.bfloat16)
 
+    parts = 4
+    tp = tr // parts
+    ups_of = jnp.where(y_at == 0, 3, jnp.where(y_at == yn - 1, 1, 2))
+
     def az(head, chunk, kind):
         at = pl.ds(chunk * tr, tr)
-        low, high = pl.ds(chunk * tr, half), pl.ds(chunk * tr + half, half)
-        src, dst, to = [
-            (ag.at[0, head, at], ag.at[1, head, at], z_up),
-            (ag.at[0, head, at], ag.at[3, head, at], z_down),
-            (ag.at[1, head, low], ag.at[2, head, low], z_up),
-            (ag.at[3, head, high], ag.at[2, head, high], z_down),
-        ][kind]
+        if kind == 0:
+            src, dst, to = ag.at[0, head, at], ag.at[1, head, at], z_up
+        elif kind == 1:
+            src, dst, to = ag.at[0, head, at], ag.at[3, head, at], z_down
+        else:
+            at = pl.ds(chunk * tr + (kind - 2) * tp, tp)
+            upward = kind - 2 < ups_of
+            src = ag.at[jnp.where(upward, 1, 3), head, at]
+            dst, to = ag.at[2, head, at], jnp.where(upward, z_up, z_down)
         return remote(src, dst, az_s.at[head, chunk, kind], az_r.at[head, chunk, kind], {"zh": to})
 
     def z_relay(head, chunk):
         for kind in (0, 1):
             az(head, chunk, kind).wait_recv()
-            go(az(head, chunk, kind + 2))
+        for i in range(parts):
+            go(az(head, chunk, 2 + i))
 
     def z_direct(head, chunk):
         go(az(head, chunk, 0))
@@ -208,15 +231,16 @@
 
     def arrive(slot, *pieces):
         for p in pieces:
-            piece(p, slot).wait_recv()
+            where(gets[slot], piece(p, slot).wait_recv)
             if slot == NEAR:
-                go(piece(p, RELAY))
+                go(piece(p, RELAY), gives[RELAY])
 
     attn(OWN, 0, first=True)
     arrive(PARTNER, IDS, 0, 1)
     attn(PARTNER, 0)
     wz[0].wait_recv()
     go(wz[3])
+    send_pieces(2, 3)
     arrive(NEAR, IDS, 0, 1)
     attn(NEAR, 0)
     arrive(FAR, IDS, 0, 1)
@@ -225,8 +249,8 @@
     attn(RELAY, 0)
     for c in range(CH):
         finish(0, c)
-        z_direct(0, c)
-
+        if c < 3:
+            z_direct(0, c)
     for copy in wz[1:]:
         copy.wait_recv()
     go(w_step("up", 0))
@@ -236,9 +260,7 @@
     attn(OWN, 1, first=True)
     arrive(PARTNER, 2, 3)
     attn(PARTNER, 1)
-    z_relay(0, 0)
     attn(NEAR, 1)
-    z_relay(0, 1)
     arrive(FAR, 2, 3)
     attn(FAR, 1)
     w_advance(0)
@@ -246,15 +268,20 @@
     attn(RELAY, 1)
     for c in range(CH):
         finish(1, c)
-        if c < 2:
-            z_direct(1, c)
+    z_relay(0, 0)
+    z_direct(1, 0)
+    z_relay(0, 1)
+    z_direct(1, 1)
+    w_advance(1)
+    z_relay(1, 0)
+    z_direct(0, 3)
     z_relay(0, 2)
-    w_advance(1)
+    w_advance(2)
+    z_relay(1, 1)
+    z_direct(1, 2)
+    w_advance(3)
     z_relay(0, 3)
-    for t in range(2, max(ups, 4)):
-        w_advance(t)
-        z_relay(1, t - 2)
-        z_direct(1, t)
+    z_direct(1, 3)
     w_local.wait()
     for t in range(yn):
         w_step("partner", t).wait_recv()
@@ -262,7 +289,7 @@
     def project(c):
         at = pl.ds(c * tr, tr)
         for head in range(2):
-            for kind in (2, 3):
+            for kind in range(2, 2 + parts):
                 az(head, c, kind).wait_recv()
         total = None
         for head in range(2):
@@ -273,18 +300,13 @@
             )
             term = jnp.dot(left, right, preferred_element_type=jnp.float32)
             total = term if total is None else total + term
-        total = total.astype(jnp.bfloat16)
-        for x in range(xn):
-            start = (x * own // HD) * HD
-            xs[c, x] = total[:, start:start + win]
+        xs[c] = jnp.transpose(total).astype(jnp.bfloat16).reshape(xn, own, tr)
         for r in range(1, xn):
             go(x_copy(c, r))
 
     def x_copy(c, r):
         to = lax.rem(x_at + r, xn)
         return remote(xs.at[c, to], xr.at[c, r - 1], x_s.at[c, r - 1], x_r.at[c, r - 1], {"x": to})
-
-    odd = lax.rem(x_at, 2) == 1
 
     def out_copy(c):
         return pltpu.make_async_copy(ot.at[c], out_hbm.at[:, pl.ds(c * tr, tr)], o_s.at[c])
@@ -294,9 +316,7 @@
         for r in range(1, xn):
             x_copy(c, r).wait_recv()
             total = total + xr[c, r - 1].astype(jnp.float32)
-        total = jnp.transpose(total)
-        mixed = jnp.where(odd, total[win - own:], total[:own])
-        ot[c] = mixed.astype(jnp.bfloat16)
+        ot[c] = total.astype(jnp.bfloat16)
         out_copy(c).start()
 
     project(0)
@@ -309,8 +329,8 @@
     project(3)
     mix(2)
     mix(3)
-    for copy in sent:
-        copy.wait_send()
+    for copy, condition in sent:
+        where(condition, copy.wait_send)
     for c in range(CH):
         out_copy(c).wait()
 
@@ -319,7 +339,6 @@
     rows = queries.shape[0]
     depth, features = out_weight.shape
     own = features // (ZH * xn)
-    win = -(-own // HD) * HD
     slab = features // ZH
     wb = depth // (2 * yn)
     ids = segment_ids.reshape(1, rows)
@@ -344,15 +363,15 @@
             pltpu.VMEM((ZH, 2, rows, HD), bf16),
             pltpu.VMEM((2 * yn, ZH, wb, slab), bf16),
             pltpu.VMEM((wb, slab), bf16),
-            pltpu.VMEM((CH, xn, rows // CH, win), bf16),
-            pltpu.VMEM((CH, xn - 1, rows // CH, win), bf16),
+            pltpu.VMEM((CH, xn, own, rows // CH), bf16),
+            pltpu.VMEM((CH, xn - 1, own, rows // CH), bf16),
             pltpu.VMEM((CH, own, rows // CH), bf16),
             dma((5, 4)), dma((5, 4)),
             dma((4,)), dma((4,)),
             dma((ups,)), dma((ups,)),
             dma((downs,)), dma((downs,)),
             dma((yn,)), dma((yn,)),
-            dma((2, CH, 4)), dma((2, CH, 4)),
+            dma((2, CH, 6)), dma((2, CH, 6)),
             dma((CH, xn - 1)), dma((CH, xn - 1)),
             dma((CH,)), dma((7,)),
         ],

time: 87.1 us -> 79.7 us (0.915)
  the two profiles are of different devices: /device:TPU:80 before, /device:TPU:64 now
where the time goes in v3:
time: 79.7 us; the launch traced here: 79.6 us
  Pallas kernels  77.8 us (98%)
  local copies, waits for them, and re-layouts  1.72 us (2%)
    pallas_call x1, Pallas kernels, shards(): pl.pallas_call(functools.partial(kernel, yn, xn), out_shape=jax.ShapeDtyp...  77.8 us
    unnamed x1, local copies, waits for them, and re-layouts  1.72 us

profile of v3, /device:TPU:64, one launch (start us, length us, event | category | flops | bytes accessed | tf_op | source)
XLA Modules:
  0.0 79.6 jit_solution(9973627867229806959)
XLA Ops:
  0.0 77.8 %shard_map.55 = bf16[320,512]{1,0:T(8,128)(2,1)} custom-call(bf16[512,256]{1,0:T(8,128)(2,1)} %q_hbm.1, bf16[512,256]{1,0:T(8,128)(2,1)} %k_hbm.1, bf16[512,256]{1,0:T(8,128)(2,1)} %v_hbm.1, s32[1,512]{1,0:T(1,128)} %bitcast.5, bf16[16,16,5120]{2,1,0:T(8,128)(2,1)} %bitcast.3), custom_call_target="tpu_custom_call" | custom-call | tf_op jit(solution)/shard_map/pallas_call | solution.py:350
  77.9 1.7 %copy.7 = bf16[512,320]{0,1:T(8,128)(2,1)} copy(bf16[512,320]{0,1:T(8,128)(2,1)} %bitcast.4) | data formatting | bytes 655360

commit v4 on v3

--- a/solution.py
+++ b/solution.py
@@ -16,7 +16,6 @@
 NEG = -1e30
 MESH = pl.DeviceIdType.MESH
 NEAR, FAR, PARTNER, RELAY, OWN = range(5)
-IDS = 4
 
 
 def tile_lanes(x, n):
@@ -26,7 +25,7 @@
 def kernel(
     yn, xn, q_hbm, k_hbm, v_hbm, ids_hbm, w_hbm, out_hbm,
     qv, kv, idr, qid, m_sc, l_sc, acc_sc, ag, wg, wrelay, xs, xr, ot,
-    kv_s, kv_r, wz_s, wz_r, wp_s, wp_r, wm_s, wm_r, wq_s, wq_r, az_s, az_r, x_s, x_r, o_s, loc,
+    kv_s, kv_r, id_s, id_r, wz_s, wz_r, w_s, wp_r, wm_r, wq_r, az_s, az_r, x_s, x_r, o_s, loc,
 ):
     rows = q_hbm.shape[0]
     tr = rows // CH
@@ -63,10 +62,11 @@
             device_id=device, device_id_type=MESH,
         )
 
-    sent = []
-
     outer = jnp.logical_and(s_at + sgn >= 0, s_at + sgn < sn)
     inner = jnp.logical_and(s_at - 2 * sgn >= 0, s_at - 2 * sgn < sn)
+    gives = {NEAR: outer, FAR: inner, PARTNER: None, RELAY: outer}
+    gets = {NEAR: outer, FAR: outer, PARTNER: None, RELAY: inner, OWN: None}
+    targets = {NEAR: {"seq": near}, FAR: {"seq": far_to}, PARTNER: {"seq": partner}, RELAY: {"seq": partner}}
 
     def where(condition, act):
         if condition is None:
@@ -74,34 +74,34 @@
         else:
             pl.when(condition)(act)
 
-    def go(copy, condition=None):
-        where(condition, copy.start)
-        sent.append((copy, condition))
+    def taken(ref, sem):
+        return remote(ref, ref, sem, sem, {"seq": partner}).wait_recv
+
+    def given(ref, sem):
+        return remote(ref, ref, sem, sem, {"seq": partner}).wait_send
 
     def piece_src(p):
-        if p == IDS:
-            return ids_hbm
         src = k_hbm if p % 2 == 0 else v_hbm
         return src.at[:, pl.ds((p // 2) * HD, HD)]
 
-    def piece_dst(p, slot):
-        return idr.at[slot] if p == IDS else kv.at[slot, p]
-
-    targets = {NEAR: {"seq": near}, FAR: {"seq": far_to}, PARTNER: {"seq": partner}, RELAY: {"seq": partner}}
-
-    gives = {NEAR: outer, FAR: inner, PARTNER: None, RELAY: outer}
-    gets = {NEAR: outer, FAR: outer, PARTNER: None, RELAY: inner, OWN: None}
-
     def piece(p, slot):
-        src = piece_dst(p, NEAR) if slot == RELAY else piece_src(p)
-        return remote(src, piece_dst(p, slot), kv_s.at[p, slot], kv_r.at[p, slot], targets[slot])
+        return remote(piece_src(p), kv.at[slot, p], kv_s.at[slot], kv_r.at[slot, p // 2], targets[slot])
+
+    def relayed(head):
+        pair = pl.ds(2 * head, 2)
+        return remote(kv.at[NEAR, pair], kv.at[RELAY, pair], kv_s.at[RELAY], kv_r.at[RELAY, head], targets[RELAY])
+
+    def marks(slot):
+        src = idr.at[NEAR] if slot == RELAY else ids_hbm
+        return remote(src, idr.at[slot], id_s.at[slot], id_r.at[slot], targets[slot])
 
     def cols(z):
         return pl.ds(pl.multiple_of(z * slab, 128), slab)
 
-    local = [pltpu.make_async_copy(piece_src(p), piece_dst(p, OWN), loc.at[p]) for p in range(5)]
-    local.append(pltpu.make_async_copy(q_hbm, qv, loc.at[5]))
-    w_local = pltpu.make_async_copy(w_hbm.at[:, :, cols(z_at)], wg.at[:, 0], loc.at[6])
+    local = [pltpu.make_async_copy(piece_src(p), kv.at[OWN, p], loc.at[0]) for p in range(4)]
+    local.append(pltpu.make_async_copy(ids_hbm, idr.at[OWN], loc.at[1]))
+    local.append(pltpu.make_async_copy(q_hbm, qv, loc.at[2]))
+    w_local = pltpu.make_async_copy(w_hbm.at[:, :, cols(z_at)], wg.at[:, 0], loc.at[3])
     for copy in local:
         copy.start()
     w_local.start()
@@ -114,33 +114,37 @@
         pl.semaphore_signal(barrier, inc=1, device_id=peer, device_id_type=MESH)
     pl.semaphore_wait(barrier, len(peers))
 
-    by = jnp.where(core == 0, z_up, z_down)
+    upper, lower = y_at == yn - 1, y_at == 0
+    by = jnp.where(jnp.logical_or(lower, jnp.logical_and(core == 0, jnp.logical_not(upper))), z_up, z_down)
     wz = [
         remote(w_hbm.at[me_block, :, cols(z_two)], wrelay, wz_s.at[0], wz_r.at[0], {"zh": by}),
-        remote(w_hbm.at[me_block, :, cols(z_up)], wg.at[me_block, 1], wz_s.at[1], wz_r.at[1], {"zh": z_up}),
-        remote(w_hbm.at[me_block, :, cols(z_down)], wg.at[me_block, 3], wz_s.at[2], wz_r.at[2], {"zh": z_down}),
-        remote(wrelay, wg.at[me_block, 2], wz_s.at[3], wz_r.at[3], {"zh": by}),
+        remote(w_hbm.at[me_block, :, cols(z_up)], wg.at[me_block, 1], wz_s.at[0], wz_r.at[1], {"zh": z_up}),
+        remote(w_hbm.at[me_block, :, cols(z_down)], wg.at[me_block, 3], wz_s.at[0], wz_r.at[1], {"zh": z_down}),
+        remote(wrelay, wg.at[me_block, 2], wz_s.at[0], wz_r.at[1], {"zh": by}),
     ]
 
     def send_pieces(*pieces):
         for p in pieces:
             for slot in (NEAR, FAR, PARTNER):
-                go(piece(p, slot), gives[slot])
-
-    go(wz[0])
-    send_pieces(IDS, 0, 1)
-    go(wz[1])
-    go(wz[2])
-
-    for copy in local:
+                where(gives[slot], piece(p, slot).start)
+
+    wz[0].start()
+    for slot in (NEAR, FAR, PARTNER):
+        where(gives[slot], marks(slot).start)
+    send_pieces(0, 1)
+    wz[1].start()
+    wz[2].start()
+
+    pltpu.make_async_copy(kv.at[OWN], kv.at[OWN], loc.at[0]).wait()
+    for copy in local[4:]:
         copy.wait()
     for i in range(rows // 128):
         wide = jnp.broadcast_to(idr[OWN, 0:1, i * 128:(i + 1) * 128].astype(jnp.float32), (128, 128))
         qid[i * 128:(i + 1) * 128, :] = jnp.transpose(wide)
 
-    def attn(slot, head, first=False):
-        def body(t, carry):
-            at = pl.ds(pl.multiple_of(t * tr, tr), tr)
+    def attn(slot, head, chunks=range(CH), first=False):
+        def body(t):
+            at = pl.ds(t * tr, tr)
             q = qv[at, head * HD:(head + 1) * HD]
             scores = lax.dot_general(
                 q, kv[slot, 2 * head], (((1,), (1,)), ((), ())), preferred_element_type=jnp.float32
@@ -165,10 +169,10 @@
             m_sc[at, :] = top
             l_sc[at, :] = part
             acc_sc[at, :] = summed
-            return carry
 
         def run():
-            lax.fori_loop(0, CH, body, 0, unroll=True)
+            for t in chunks:
+                body(t)
 
         where(gets[slot], run)
 
@@ -179,10 +183,11 @@
 
     parts = 4
     tp = tr // parts
-    ups_of = jnp.where(y_at == 0, 3, jnp.where(y_at == yn - 1, 1, 2))
+    ups_of = jnp.where(lower, 3, jnp.where(upper, 1, 2))
 
     def az(head, chunk, kind):
         at = pl.ds(chunk * tr, tr)
+        arrived = az_r.at[head, chunk, 0]
         if kind == 0:
             src, dst, to = ag.at[0, head, at], ag.at[1, head, at], z_up
         elif kind == 1:
@@ -192,105 +197,108 @@
             upward = kind - 2 < ups_of
             src = ag.at[jnp.where(upward, 1, 3), head, at]
             dst, to = ag.at[2, head, at], jnp.where(upward, z_up, z_down)
-        return remote(src, dst, az_s.at[head, chunk, kind], az_r.at[head, chunk, kind], {"zh": to})
+            arrived = az_r.at[head, chunk, 1]
+        return remote(src, dst, az_s.at[0], arrived, {"zh": to})
 
     def z_relay(head, chunk):
-        for kind in (0, 1):
-            az(head, chunk, kind).wait_recv()
+        at = pl.ds(chunk * tr, tr)
+        taken(ag.at[pl.ds(0, 2), head, at], az_r.at[head, chunk, 0])()
         for i in range(parts):
-            go(az(head, chunk, 2 + i))
+            az(head, chunk, 2 + i).start()
 
     def z_direct(head, chunk):
-        go(az(head, chunk, 0))
-        go(az(head, chunk, 1))
+        az(head, chunk, 0).start()
+        az(head, chunk, 1).start()
 
     ups, downs = yn // 2, (yn - 1) // 2
 
     def w_step(kind, t):
         if kind == "up":
-            src, sems, to = wblock(-t), (wp_s.at[t], wp_r.at[t]), y_up
+            src, arrived, to = wblock(-t), wp_r.at[t], y_up
         elif kind == "down":
-            src, sems, to = wblock(t), (wm_s.at[t], wm_r.at[t]), y_down
+            src, arrived, to = wblock(t), wm_r.at[t], y_down
         else:
-            src, sems, to = wblock(t), (wq_s.at[t % yn], wq_r.at[t % yn]), partner
+            src, arrived, to = wblock(t), wq_r.at[0], partner
         block = wg.at[src, pl.ds(1, ZH - 1)]
-        return remote(block, block, *sems, {"seq": to})
+        return remote(block, block, w_s.at[0], arrived, {"seq": to})
 
     def w_advance(t):
         if t >= ups:
             return
         w_step("up", t).wait_recv()
         if t + 1 < ups:
-            go(w_step("up", t + 1))
-        go(w_step("partner", -1 - t))
+            w_step("up", t + 1).start()
+        w_step("partner", -1 - t).start()
         if t < downs:
             w_step("down", t).wait_recv()
             if t + 1 < downs:
-                go(w_step("down", t + 1))
-            go(w_step("partner", 1 + t))
-
-    def arrive(slot, *pieces):
-        for p in pieces:
-            where(gets[slot], piece(p, slot).wait_recv)
+                w_step("down", t + 1).start()
+            w_step("partner", 1 + t).start()
+
+    def arrive(slot, head):
+        def act():
+            if head == 0:
+                marks(slot).wait_recv()
+                if slot == NEAR:
+                    marks(RELAY).start()
+            taken(kv.at[slot, pl.ds(2 * head, 2)], kv_r.at[slot, head])()
             if slot == NEAR:
-                go(piece(p, RELAY), gives[RELAY])
+                relayed(head).start()
+
+        where(gets[slot], act)
 
     attn(OWN, 0, first=True)
-    arrive(PARTNER, IDS, 0, 1)
+    arrive(PARTNER, 0)
     attn(PARTNER, 0)
     wz[0].wait_recv()
-    go(wz[3])
-    send_pieces(2, 3)
-    arrive(NEAR, IDS, 0, 1)
+    wz[3].start()
+    send_pieces(2)
+    arrive(NEAR, 0)
     attn(NEAR, 0)
-    arrive(FAR, IDS, 0, 1)
-    attn(FAR, 0)
-    arrive(RELAY, IDS, 0, 1)
-    attn(RELAY, 0)
+    taken(wg.at[me_block, pl.ds(1, ZH - 1)], wz_r.at[1])()
+    w_step("up", 0).start()
+    w_step("down", 0).start()
+    w_step("partner", 0).start()
+    send_pieces(3)
+    arrive(FAR, 0)
+    arrive(RELAY, 0)
     for c in range(CH):
+        attn(FAR, 0, (c,))
+        attn(RELAY, 0, (c,))
         finish(0, c)
-        if c < 3:
-            z_direct(0, c)
-    for copy in wz[1:]:
-        copy.wait_recv()
-    go(w_step("up", 0))
-    go(w_step("down", 0))
-    go(w_step("partner", 0))
-    arrive(NEAR, 2, 3)
+        z_direct(0, c)
+    w_advance(0)
     attn(OWN, 1, first=True)
-    arrive(PARTNER, 2, 3)
+    arrive(PARTNER, 1)
     attn(PARTNER, 1)
+    arrive(NEAR, 1)
     attn(NEAR, 1)
-    arrive(FAR, 2, 3)
+    z_relay(0, 0)
+    arrive(FAR, 1)
     attn(FAR, 1)
-    w_advance(0)
-    arrive(RELAY, 2, 3)
-    attn(RELAY, 1)
+    w_advance(1)
+    z_relay(0, 1)
+    arrive(RELAY, 1)
     for c in range(CH):
+        attn(RELAY, 1, (c,))
         finish(1, c)
-    z_relay(0, 0)
-    z_direct(1, 0)
-    z_relay(0, 1)
-    z_direct(1, 1)
-    w_advance(1)
+        if c < 2:
+            z_direct(1, c)
+    w_advance(2)
+    z_relay(0, 2)
     z_relay(1, 0)
-    z_direct(0, 3)
-    z_relay(0, 2)
-    w_advance(2)
-    z_relay(1, 1)
     z_direct(1, 2)
     w_advance(3)
     z_relay(0, 3)
+    z_relay(1, 1)
     z_direct(1, 3)
     w_local.wait()
-    for t in range(yn):
-        w_step("partner", t).wait_recv()
+    taken(wg.at[pl.ds(0, yn), pl.ds(1, ZH - 1)], wq_r.at[0])()
 
     def project(c):
         at = pl.ds(c * tr, tr)
         for head in range(2):
-            for kind in range(2, 2 + parts):
-                az(head, c, kind).wait_recv()
+            taken(ag.at[2, head, at], az_r.at[head, c, 1])()
         total = None
         for head in range(2):
             left = jnp.concatenate([ag[r, head, at, :] for r in range(ZH)], axis=1)
@@ -302,19 +310,19 @@
             total = term if total is None else total + term
         xs[c] = jnp.transpose(total).astype(jnp.bfloat16).reshape(xn, own, tr)
         for r in range(1, xn):
-            go(x_copy(c, r))
+            x_copy(c, r).start()
 
     def x_copy(c, r):
         to = lax.rem(x_at + r, xn)
-        return remote(xs.at[c, to], xr.at[c, r - 1], x_s.at[c, r - 1], x_r.at[c, r - 1], {"x": to})
+        return remote(xs.at[c, to], xr.at[c, r - 1], x_s.at[0], x_r.at[c], {"x": to})
 
     def out_copy(c):
-        return pltpu.make_async_copy(ot.at[c], out_hbm.at[:, pl.ds(c * tr, tr)], o_s.at[c])
+        return pltpu.make_async_copy(ot.at[c], out_hbm.at[:, pl.ds(c * tr, tr)], o_s.at[0])
 
     def mix(c):
         total = xs[c, x_at].astype(jnp.float32)
+        taken(xr.at[c], x_r.at[c])()
         for r in range(1, xn):
-            x_copy(c, r).wait_recv()
             total = total + xr[c, r - 1].astype(jnp.float32)
         ot[c] = total.astype(jnp.bfloat16)
         out_copy(c).start()
@@ -329,10 +337,14 @@
     project(3)
     mix(2)
     mix(3)
-    for copy, condition in sent:
-        where(condition, copy.wait_send)
-    for c in range(CH):
-        out_copy(c).wait()
+    for slot in (NEAR, FAR, PARTNER, RELAY):
+        where(gives[slot], marks(slot).wait_send)
+        where(gives[slot], given(kv.at[slot], kv_s.at[slot]))
+    given(wg.at[0], wz_s.at[0])()
+    given(wg.at[pl.ds(0, 2 * yn - 1), pl.ds(1, ZH - 1)], w_s.at[0])()
+    given(ag.at[pl.ds(0, 3)], az_s.at[0])()
+    given(xr, x_s.at[0])()
+    pltpu.make_async_copy(ot, ot, o_s.at[0]).wait()
 
 
 def shards(yn, xn, queries, keys, values, segment_ids, out_weight):
@@ -366,14 +378,12 @@
             pltpu.VMEM((CH, xn, own, rows // CH), bf16),
             pltpu.VMEM((CH, xn - 1, own, rows // CH), bf16),
             pltpu.VMEM((CH, own, rows // CH), bf16),
-            dma((5, 4)), dma((5, 4)),
-            dma((4,)), dma((4,)),
-            dma((ups,)), dma((ups,)),
-            dma((downs,)), dma((downs,)),
-            dma((yn,)), dma((yn,)),
-            dma((2, CH, 6)), dma((2, CH, 6)),
-            dma((CH, xn - 1)), dma((CH, xn - 1)),
-            dma((CH,)), dma((7,)),
+            dma((4,)), dma((4, 2)), dma((4,)), dma((4,)),
+            dma((1,)), dma((2,)),
+            dma((1,)), dma((ups,)), dma((downs,)), dma((1,)),
+            dma((1,)), dma((2, CH, 2)),
+            dma((1,)), dma((CH,)),
+            dma((1,)), dma((4,)),
         ],
         compiler_params=pltpu.CompilerParams(
             collective_id=0, has_side_effects=True, vmem_limit_bytes=60 * 1024 * 1024

time: 79.7 us -> 75.6 us (0.949)
  the two profiles are of different devices: /device:TPU:64 before, /device:TPU:1 now
where the time goes in v4:
time: 75.6 us; the launch traced here: 74.6 us
  Pallas kernels  72.8 us (96%)
  local copies, waits for them, and re-layouts  1.72 us (2%)
    pallas_call x1, Pallas kernels, shards(): pl.pallas_call(functools.partial(kernel, yn, xn), out_shape=jax.ShapeDtyp...  72.8 us
    unnamed x1, local copies, waits for them, and re-layouts  1.72 us

profile of v4, /device:TPU:1, one launch (start us, length us, event | category | flops | bytes accessed | tf_op | source)
XLA Modules:
  0.0 74.6 jit_solution(977050310146699019)
XLA Ops:
  0.0 72.8 %shard_map.55 = bf16[320,512]{1,0:T(8,128)(2,1)} custom-call(bf16[512,256]{1,0:T(8,128)(2,1)} %q_hbm.1, bf16[512,256]{1,0:T(8,128)(2,1)} %k_hbm.1, bf16[512,256]{1,0:T(8,128)(2,1)} %v_hbm.1, s32[1,512]{1,0:T(1,128)} %bitcast.5, bf16[16,16,5120]{2,1,0:T(8,128)(2,1)} %bitcast.3), custom_call_target="tpu_custom_call" | custom-call | tf_op jit(solution)/shard_map/pallas_call | solution.py:362
  72.9 1.7 %copy.7 = bf16[512,320]{0,1:T(8,128)(2,1)} copy(bf16[512,320]{0,1:T(8,128)(2,1)} %bitcast.4) | data formatting | bytes 655360

commit v5 on v4

--- a/solution.py
+++ b/solution.py
@@ -24,13 +24,13 @@
 
 def kernel(
     yn, xn, q_hbm, k_hbm, v_hbm, ids_hbm, w_hbm, out_hbm,
-    qv, kv, idr, qid, m_sc, l_sc, acc_sc, ag, wg, wrelay, xs, xr, ot,
+    qv, kv, idr, qid, m_sc, l_sc, acc_sc, ag, wg, wrelay, xs,
     kv_s, kv_r, id_s, id_r, wz_s, wz_r, w_s, wp_r, wm_r, wq_r, az_s, az_r, x_s, x_r, o_s, loc,
 ):
     rows = q_hbm.shape[0]
     tr = rows // CH
     slab = w_hbm.shape[2] // ZH
-    own = out_hbm.shape[0]
+    own = out_hbm.shape[1]
     factor = HD ** -0.5 * math.log2(math.e)
 
     s_at = lax.axis_index("seq")
@@ -102,16 +102,15 @@
     local.append(pltpu.make_async_copy(ids_hbm, idr.at[OWN], loc.at[1]))
     local.append(pltpu.make_async_copy(q_hbm, qv, loc.at[2]))
     w_local = pltpu.make_async_copy(w_hbm.at[:, :, cols(z_at)], wg.at[:, 0], loc.at[3])
-    for copy in local:
-        copy.start()
-    w_local.start()
-
     barrier = pltpu.get_barrier_semaphore()
     peers = [{"seq": near}, {"seq": partner}, {"seq": far_to}, {"seq": far_from}, {"seq": y_up}, {"seq": y_down},
              {"zh": z_up}, {"zh": z_down}]
     peers += [{"x": lax.rem(x_at + r, xn)} for r in range(1, xn)]
     for peer in peers:
         pl.semaphore_signal(barrier, inc=1, device_id=peer, device_id_type=MESH)
+    for copy in local:
+        copy.start()
+    w_local.start()
     pl.semaphore_wait(barrier, len(peers))
 
     upper, lower = y_at == yn - 1, y_at == 0
@@ -181,30 +180,24 @@
         total = jnp.sum(l_sc[at, :], axis=1, keepdims=True)
         ag[0, head, at, :] = (acc_sc[at, :] / total).astype(jnp.bfloat16)
 
-    parts = 4
-    tp = tr // parts
-    ups_of = jnp.where(lower, 3, jnp.where(upper, 1, 2))
+    def turn(chunk):
+        return jnp.where(upper, 1 - chunk % 2, chunk % 2)
 
     def az(head, chunk, kind):
         at = pl.ds(chunk * tr, tr)
-        arrived = az_r.at[head, chunk, 0]
-        if kind == 0:
-            src, dst, to = ag.at[0, head, at], ag.at[1, head, at], z_up
-        elif kind == 1:
-            src, dst, to = ag.at[0, head, at], ag.at[3, head, at], z_down
-        else:
-            at = pl.ds(chunk * tr + (kind - 2) * tp, tp)
-            upward = kind - 2 < ups_of
-            src = ag.at[jnp.where(upward, 1, 3), head, at]
-            dst, to = ag.at[2, head, at], jnp.where(upward, z_up, z_down)
-            arrived = az_r.at[head, chunk, 1]
-        return remote(src, dst, az_s.at[0], arrived, {"zh": to})
+        way = turn(chunk) if kind == 2 else kind
+        rel, to = 1 + 2 * way, jnp.where(way == 0, z_up, z_down)
+        src, dst = (rel, 2) if kind == 2 else (0, rel)
+        return remote(
+            ag.at[src, head, at], ag.at[dst, head, at], az_s.at[0], az_r.at[head, chunk, kind], {"zh": to}
+        )
+
+    def came(head, chunk, way):
+        taken(ag.at[0, head, pl.ds(chunk * tr, tr)], az_r.at[head, chunk, way])()
 
     def z_relay(head, chunk):
-        at = pl.ds(chunk * tr, tr)
-        taken(ag.at[pl.ds(0, 2), head, at], az_r.at[head, chunk, 0])()
-        for i in range(parts):
-            az(head, chunk, 2 + i).start()
+        came(head, chunk, turn(chunk))
+        az(head, chunk, 2).start()
 
     def z_direct(head, chunk):
         az(head, chunk, 0).start()
@@ -266,31 +259,34 @@
         attn(FAR, 0, (c,))
         attn(RELAY, 0, (c,))
         finish(0, c)
-        z_direct(0, c)
-    w_advance(0)
+        if c < 3:
+            z_direct(0, c)
     attn(OWN, 1, first=True)
     arrive(PARTNER, 1)
     attn(PARTNER, 1)
+    w_advance(0)
+    z_relay(0, 0)
     arrive(NEAR, 1)
-    attn(NEAR, 1)
-    z_relay(0, 0)
     arrive(FAR, 1)
-    attn(FAR, 1)
-    w_advance(1)
-    z_relay(0, 1)
     arrive(RELAY, 1)
     for c in range(CH):
+        attn(NEAR, 1, (c,))
+        attn(FAR, 1, (c,))
         attn(RELAY, 1, (c,))
         finish(1, c)
         if c < 2:
             z_direct(1, c)
+        if c == 1:
+            z_relay(0, 1)
+            w_advance(1)
     w_advance(2)
+    z_relay(1, 0)
+    z_direct(0, 3)
     z_relay(0, 2)
-    z_relay(1, 0)
     z_direct(1, 2)
     w_advance(3)
+    z_relay(1, 1)
     z_relay(0, 3)
-    z_relay(1, 1)
     z_direct(1, 3)
     w_local.wait()
     taken(wg.at[pl.ds(0, yn), pl.ds(1, ZH - 1)], wq_r.at[0])()
@@ -298,7 +294,8 @@
     def project(c):
         at = pl.ds(c * tr, tr)
         for head in range(2):
-            taken(ag.at[2, head, at], az_r.at[head, c, 1])()
+            came(head, c, 1 - turn(c))
+            az(head, c, 2).wait_recv()
         total = None
         for head in range(2):
             left = jnp.concatenate([ag[r, head, at, :] for r in range(ZH)], axis=1)
@@ -311,40 +308,33 @@
         xs[c] = jnp.transpose(total).astype(jnp.bfloat16).reshape(xn, own, tr)
         for r in range(1, xn):
             x_copy(c, r).start()
+        own_copy(c).start()
+
+    def block(c):
+        return pl.ds(c * tr, tr)
 
     def x_copy(c, r):
         to = lax.rem(x_at + r, xn)
-        return remote(xs.at[c, to], xr.at[c, r - 1], x_s.at[0], x_r.at[c], {"x": to})
-
-    def out_copy(c):
-        return pltpu.make_async_copy(ot.at[c], out_hbm.at[:, pl.ds(c * tr, tr)], o_s.at[0])
-
-    def mix(c):
-        total = xs[c, x_at].astype(jnp.float32)
-        taken(xr.at[c], x_r.at[c])()
-        for r in range(1, xn):
-            total = total + xr[c, r - 1].astype(jnp.float32)
-        ot[c] = total.astype(jnp.bfloat16)
-        out_copy(c).start()
+        return remote(xs.at[c, to], out_hbm.at[r, :, block(c)], x_s.at[0], x_r.at[0], {"x": to})
+
+    def own_copy(c):
+        return pltpu.make_async_copy(xs.at[c, x_at], out_hbm.at[0, :, block(c)], o_s.at[0])
 
     project(0)
     z_relay(1, 2)
     project(1)
     z_relay(1, 3)
-    mix(0)
     project(2)
-    mix(1)
     project(3)
-    mix(2)
-    mix(3)
+    taken(out_hbm.at[pl.ds(1, xn - 1)], x_r.at[0])()
     for slot in (NEAR, FAR, PARTNER, RELAY):
         where(gives[slot], marks(slot).wait_send)
         where(gives[slot], given(kv.at[slot], kv_s.at[slot]))
     given(wg.at[0], wz_s.at[0])()
     given(wg.at[pl.ds(0, 2 * yn - 1), pl.ds(1, ZH - 1)], w_s.at[0])()
     given(ag.at[pl.ds(0, 3)], az_s.at[0])()
-    given(xr, x_s.at[0])()
-    pltpu.make_async_copy(ot, ot, o_s.at[0]).wait()
+    given(out_hbm.at[pl.ds(1, xn - 1)], x_s.at[0])()
+    pltpu.make_async_copy(out_hbm.at[0], out_hbm.at[0], o_s.at[0]).wait()
 
 
 def shards(yn, xn, queries, keys, values, segment_ids, out_weight):
@@ -361,7 +351,7 @@
     ups, downs = yn // 2, max(1, (yn - 1) // 2)
     out = pl.pallas_call(
         functools.partial(kernel, yn, xn),
-        out_shape=jax.ShapeDtypeStruct((own, rows), bf16),
+        out_shape=jax.ShapeDtypeStruct((xn, own, rows), bf16),
         in_specs=[hbm] * 5,
         out_specs=hbm,
         scratch_shapes=[
@@ -376,20 +366,21 @@
             pltpu.VMEM((2 * yn, ZH, wb, slab), bf16),
             pltpu.VMEM((wb, slab), bf16),
             pltpu.VMEM((CH, xn, own, rows // CH), bf16),
-            pltpu.VMEM((CH, xn - 1, own, rows // CH), bf16),
-            pltpu.VMEM((CH, own, rows // CH), bf16),
             dma((4,)), dma((4, 2)), dma((4,)), dma((4,)),
             dma((1,)), dma((2,)),
             dma((1,)), dma((ups,)), dma((downs,)), dma((1,)),
-            dma((1,)), dma((2, CH, 2)),
-            dma((1,)), dma((CH,)),
+            dma((1,)), dma((2, CH, 3)),
+            dma((1,)), dma((1,)),
             dma((1,)), dma((4,)),
         ],
         compiler_params=pltpu.CompilerParams(
             collective_id=0, has_side_effects=True, vmem_limit_bytes=60 * 1024 * 1024
         ),
     )(queries, keys, values, ids, weight)
-    return jnp.transpose(out)
+    total = out[0].astype(f32)
+    for r in range(1, xn):
+        total = total + out[r].astype(f32)
+    return jnp.transpose(total.astype(bf16))
 
 
 def build(mesh, yn):

time: 75.6 us -> 74.9 us (level); the launches traced: 74.6 us -> 74.8 us
  other arithmetic: 0 us -> 2.16 us
  local copies, waits for them, and re-layouts: 1.72 us -> 0 us
    transpose x0 -> x1, other arithmetic: none -> 2.16 us  [shards(): return jnp.transpose(total.astype(bf16))]
    unnamed x1 -> x0, local copies, waits for them, and re-layouts: 1.72 us -> none
where the time goes in v5:
time: 74.9 us; the launch traced here: 74.8 us
  Pallas kernels  72.6 us (97%)
  other arithmetic  2.16 us (3%)
    pallas_call x1, Pallas kernels, shards(): pl.pallas_call(functools.partial(kernel, yn, xn), out_shape=jax.ShapeDtyp...  72.6 us
    transpose x1, other arithmetic, shards(): return jnp.transpose(total.astype(bf16))  2.16 us

profile of v5, /device:TPU:1, one launch (start us, length us, event | category | flops | bytes accessed | tf_op | source)
XLA Modules:
  0.0 74.8 jit_solution(16761520215178749222)
XLA Ops:
  0.0 72.6 %shard_map.55 = bf16[4,320,512]{2,1,0:T(8,128)(2,1)} custom-call(bf16[512,256]{1,0:T(8,128)(2,1)} %q_hbm.1, bf16[512,256]{1,0:T(8,128)(2,1)} %k_hbm.1, bf16[512,256]{1,0:T(8,128)(2,1)} %v_hbm.1, s32[1,512]{1,0:T(1,128)} %bitcast.7, bf16[16,16,5120]{2,1,0:T(8,128)(2,1)} %bitcast.6), custom_call_target="tpu_custom_call" | custom-call | tf_op jit(solution)/shard_map/pallas_call | solution.py:352
  72.6 2.2 %fusion = bf16[512,320]{0,1:T(8,128)(2,1)} fusion(bf16[4,320,512]{2,1,0:T(8,128)(2,1)} %shard_map.55), kind=kLoop, calls=%fused_computation.1 | loop fusion | flops 1310720 | bytes 1638400 | tf_op jit(solution)/shard_map/transpose | solution.py:383

commit v6 on v5

--- a/solution.py
+++ b/solution.py
@@ -24,13 +24,13 @@
 
 def kernel(
     yn, xn, q_hbm, k_hbm, v_hbm, ids_hbm, w_hbm, out_hbm,
-    qv, kv, idr, qid, m_sc, l_sc, acc_sc, ag, wg, wrelay, xs,
+    qv, kv, idr, qid, m_sc, l_sc, acc_sc, ag, wg, wrelay, xs, xr, ot,
     kv_s, kv_r, id_s, id_r, wz_s, wz_r, w_s, wp_r, wm_r, wq_r, az_s, az_r, x_s, x_r, o_s, loc,
 ):
     rows = q_hbm.shape[0]
     tr = rows // CH
     slab = w_hbm.shape[2] // ZH
-    own = out_hbm.shape[1]
+    own = out_hbm.shape[0]
     factor = HD ** -0.5 * math.log2(math.e)
 
     s_at = lax.axis_index("seq")
@@ -248,11 +248,6 @@
     send_pieces(2)
     arrive(NEAR, 0)
     attn(NEAR, 0)
-    taken(wg.at[me_block, pl.ds(1, ZH - 1)], wz_r.at[1])()
-    w_step("up", 0).start()
-    w_step("down", 0).start()
-    w_step("partner", 0).start()
-    send_pieces(3)
     arrive(FAR, 0)
     arrive(RELAY, 0)
     for c in range(CH):
@@ -261,6 +256,12 @@
         finish(0, c)
         if c < 3:
             z_direct(0, c)
+        if c == 0:
+            taken(wg.at[me_block, pl.ds(1, ZH - 1)], wz_r.at[1])()
+            w_step("up", 0).start()
+            w_step("down", 0).start()
+            w_step("partner", 0).start()
+            send_pieces(3)
     attn(OWN, 1, first=True)
     arrive(PARTNER, 1)
     attn(PARTNER, 1)
@@ -306,35 +307,39 @@
             term = jnp.dot(left, right, preferred_element_type=jnp.float32)
             total = term if total is None else total + term
         xs[c] = jnp.transpose(total).astype(jnp.bfloat16).reshape(xn, own, tr)
-        for r in range(1, xn):
+        for r in sorted(range(1, xn), key=lambda r: -min(r, xn - r)):
             x_copy(c, r).start()
-        own_copy(c).start()
-
-    def block(c):
-        return pl.ds(c * tr, tr)
 
     def x_copy(c, r):
         to = lax.rem(x_at + r, xn)
-        return remote(xs.at[c, to], out_hbm.at[r, :, block(c)], x_s.at[0], x_r.at[0], {"x": to})
-
-    def own_copy(c):
-        return pltpu.make_async_copy(xs.at[c, x_at], out_hbm.at[0, :, block(c)], o_s.at[0])
+        return remote(xs.at[c, to], xr.at[c, r - 1], x_s.at[0], x_r.at[c], {"x": to})
+
+    def mix(c):
+        taken(xr.at[c], x_r.at[c])()
+        total = xs[c, x_at].astype(jnp.float32)
+        for r in range(1, xn):
+            total = total + xr[c, r - 1].astype(jnp.float32)
+        ot[c] = total.astype(jnp.bfloat16)
+        pltpu.make_async_copy(ot.at[c], out_hbm.at[:, pl.ds(c * tr, tr)], o_s.at[0]).start()
 
     project(0)
     z_relay(1, 2)
     project(1)
     z_relay(1, 3)
+    mix(0)
     project(2)
     project(3)
-    taken(out_hbm.at[pl.ds(1, xn - 1)], x_r.at[0])()
+    mix(1)
+    mix(2)
+    mix(3)
     for slot in (NEAR, FAR, PARTNER, RELAY):
         where(gives[slot], marks(slot).wait_send)
         where(gives[slot], given(kv.at[slot], kv_s.at[slot]))
     given(wg.at[0], wz_s.at[0])()
     given(wg.at[pl.ds(0, 2 * yn - 1), pl.ds(1, ZH - 1)], w_s.at[0])()
     given(ag.at[pl.ds(0, 3)], az_s.at[0])()
-    given(out_hbm.at[pl.ds(1, xn - 1)], x_s.at[0])()
-    pltpu.make_async_copy(out_hbm.at[0], out_hbm.at[0], o_s.at[0]).wait()
+    given(xr, x_s.at[0])()
+    pltpu.make_async_copy(ot, ot, o_s.at[0]).wait()
 
 
 def shards(yn, xn, queries, keys, values, segment_ids, out_weight):
@@ -351,7 +356,7 @@
     ups, downs = yn // 2, max(1, (yn - 1) // 2)
     out = pl.pallas_call(
         functools.partial(kernel, yn, xn),
-        out_shape=jax.ShapeDtypeStruct((xn, own, rows), bf16),
+        out_shape=jax.ShapeDtypeStruct((own, rows), bf16),
         in_specs=[hbm] * 5,
         out_specs=hbm,
         scratch_shapes=[
@@ -366,21 +371,20 @@
             pltpu.VMEM((2 * yn, ZH, wb, slab), bf16),
             pltpu.VMEM((wb, slab), bf16),
             pltpu.VMEM((CH, xn, own, rows // CH), bf16),
+            pltpu.VMEM((CH, xn - 1, own, rows // CH), bf16),
+            pltpu.VMEM((CH, own, rows // CH), bf16),
             dma((4,)), dma((4, 2)), dma((4,)), dma((4,)),
             dma((1,)), dma((2,)),
             dma((1,)), dma((ups,)), dma((downs,)), dma((1,)),
             dma((1,)), dma((2, CH, 3)),
-            dma((1,)), dma((1,)),
+            dma((1,)), dma((CH,)),
             dma((1,)), dma((4,)),
         ],
         compiler_params=pltpu.CompilerParams(
             collective_id=0, has_side_effects=True, vmem_limit_bytes=60 * 1024 * 1024
         ),
     )(queries, keys, values, ids, weight)
-    total = out[0].astype(f32)
-    for r in range(1, xn):
-        total = total + out[r].astype(f32)
-    return jnp.transpose(total.astype(bf16))
+    return jnp.transpose(out)
 
 
 def build(mesh, yn):

time: 74.9 us -> 74 us (0.988)
  other arithmetic: 2.16 us -> 0 us
  local copies, waits for them, and re-layouts: 0 us -> 1.72 us
  Pallas kernels: 72.6 us -> 71.4 us
    transpose x1 -> x0, other arithmetic: 2.16 us -> none  [shards(): return jnp.transpose(total.astype(bf16))]
    unnamed x0 -> x1, local copies, waits for them, and re-layouts: none -> 1.72 us
    pallas_call x1, Pallas kernels: 72.6 us -> 71.4 us  [shards(): pl.pallas_call(functools.partial(kernel, yn, xn), out_shape=jax.ShapeDtyp...]
where the time goes in v6:
time: 74 us; the launch traced here: 73.2 us
  Pallas kernels  71.4 us (96%)
  local copies, waits for them, and re-layouts  1.72 us (2%)
    pallas_call x1, Pallas kernels, shards(): pl.pallas_call(functools.partial(kernel, yn, xn), out_shape=jax.ShapeDtyp...  71.4 us
    unnamed x1, local copies, waits for them, and re-layouts  1.72 us

profile of v6, /device:TPU:1, one launch (start us, length us, event | category | flops | bytes accessed | tf_op | source)
XLA Modules:
  0.0 73.2 jit_solution(15089075511308484588)
XLA Ops:
  0.0 71.4 %shard_map.55 = bf16[320,512]{1,0:T(8,128)(2,1)} custom-call(bf16[512,256]{1,0:T(8,128)(2,1)} %q_hbm.1, bf16[512,256]{1,0:T(8,128)(2,1)} %k_hbm.1, bf16[512,256]{1,0:T(8,128)(2,1)} %v_hbm.1, s32[1,512]{1,0:T(1,128)} %bitcast.5, bf16[16,16,5120]{2,1,0:T(8,128)(2,1)} %bitcast.3), custom_call_target="tpu_custom_call" | custom-call | tf_op jit(solution)/shard_map/pallas_call | solution.py:357
  71.4 1.7 %copy.7 = bf16[512,320]{0,1:T(8,128)(2,1)} copy(bf16[512,320]{0,1:T(8,128)(2,1)} %bitcast.4) | data formatting | bytes 655360
